TPU v7x, 32 devices: a whole 2x2x4 slice. The times are simulated.
32 devices in a mesh: ctx: 16 (over z, y, core), fsdp: 2 (over x).
Axes of the slice: x: 2, y: 2, z: 4, core: 2. Of those that a mesh axis runs over, the one named last changes fastest.
Arguments:
- hidden: bfloat16 [2, 2048, 896], P('fsdp', 'ctx'), may hold values from -8 to 8
- pair_of: int32 [16], replicated, may hold values from 0 to 15, each once
- attn_gain: bfloat16 [896], P('fsdp'), may hold values from 0.5 to 1.5
- query_weight: bfloat16 [896, 896], P('fsdp'), may hold values from -1 to 1
- query_bias: bfloat16 [896], P('fsdp'), may hold values from -3 to 3
- key_weight: bfloat16 [896, 128], P('fsdp'), may hold values from -1 to 1
- key_bias: bfloat16 [128], P('fsdp'), may hold values from -3 to 3
- value_weight: bfloat16 [896, 128], P('fsdp'), may hold values from -0.1875 to 0.1875
- value_bias: bfloat16 [128], P('fsdp'), may hold values from -0.59765625 to 0.59765625
- out_weight: bfloat16 [896, 896], P('fsdp'), may hold values from -1 to 1
- mlp_gain: bfloat16 [896], P('fsdp'), may hold values from 0.5 to 1.5
- gate_weight: bfloat16 [896, 4864], P('fsdp'), may hold values from -0.1875 to 0.1875
- up_weight: bfloat16 [896, 4864], P('fsdp'), may hold values from -0.1875 to 0.1875
- down_weight: bfloat16 [4864, 896], P('fsdp'), may hold values from -0.078125 to 0.078125
- cotangent: bfloat16 [2, 2048, 896], P('fsdp', 'ctx'), may hold values from -6 to 6
Outputs:
- output: bfloat16 [2, 2048, 896], P('fsdp', 'ctx')
- input_grad: bfloat16 [2, 2048, 896], P('fsdp', 'ctx')
- attn_gain_grad: float32 [896], P('fsdp')
- query_weight_grad: float32 [896, 896], P('fsdp')
- query_bias_grad: float32 [896], P('fsdp')
- key_weight_grad: float32 [896, 128], P('fsdp')
- key_bias_grad: float32 [128], P('fsdp')
- value_weight_grad: float32 [896, 128], P('fsdp')
- value_bias_grad: float32 [128], P('fsdp')
- out_weight_grad: float32 [896, 896], P('fsdp')
- mlp_gain_grad: float32 [896], P('fsdp')
- gate_weight_grad: float32 [896, 4864], P('fsdp')
- up_weight_grad: float32 [896, 4864], P('fsdp')
- down_weight_grad: float32 [4864, 896], P('fsdp')
Inputs may be any that keep to these rules, and one draw needn't show every extreme that they name: A permutation: index c of ctx holds sequence blocks pair_of[c] and 31 - pair_of[c], each of 64 tokens.
All inputs are finite; a program needn't handle non-finite values.
Results may differ from a plain program's by a relative error of at most 0.034.
Values may be sent and summed in bfloat16 or wider, within the bound.
No kernel may reach another device: no remote copies, remote signals or barrier semaphores. Data moves between devices by JAX's collectives and lax.ppermute only.
A program may use at most 320 MiB of HBM per device.

v0:
```python
import math

import jax
import jax.numpy as jnp
from jax import lax
from jax.sharding import PartitionSpec as P

H = 14
KVH = 2
HD = 64


EPSILON = 1e-06
THETA_BASE = 1000000.0


def rotate_half(values):
    middle = values.shape[-1] // 2
    return jnp.concatenate([-values[..., middle:], values[..., :middle]], -1)


def rotate_back(values):
    middle = values.shape[-1] // 2
    return jnp.concatenate([values[..., middle:], -values[..., :middle]], -1)


def rotary(values, cosine, sine):
    return values * cosine + rotate_half(values) * sine


def rotary_back(values, cosine, sine):
    return values * cosine + rotate_back(values * sine)


def rotary_tables(positions):
    middle = HD // 2
    freqs = jnp.power(THETA_BASE, -2.0 * jnp.arange(middle, dtype=jnp.float32) / HD)
    angle = positions.astype(jnp.float32)[:, None] * freqs[None, :]
    angle = jnp.concatenate([angle, angle], -1)[:, None, :]
    return (jnp.cos(angle), jnp.sin(angle))


def normalize(values, gain):
    inverse = lax.rsqrt(jnp.mean(values * values, -1, keepdims=True) + EPSILON)
    return (values * inverse * gain, inverse)


def norm_back(values, inverse, gain, grad):
    scaled = gain * grad
    mean_term = jnp.mean(scaled * values, -1, keepdims=True)
    grad_values = inverse * scaled - values * inverse**3 * mean_term
    grad_gain = jnp.sum((grad * values * inverse).reshape(-1, values.shape[-1]), 0)
    return (grad_values, grad_gain)


def project(left, weight, bias):
    return jnp.einsum(
        "srd,de->sre", left, weight, preferred_element_type=jnp.float32
    ) + bias.astype(jnp.float32)


def to_sequence(gathered, holder, n_ctx, half_rows):
    seq_count, model_cols = (gathered.shape[0], gathered.shape[2])
    blocks = gathered.reshape(seq_count, n_ctx, 2, half_rows, model_cols)
    first_half = jnp.take(blocks[:, :, 0], holder, axis=1)
    second_half = jnp.take(blocks[:, :, 1], holder[::-1], axis=1)
    return jnp.concatenate([first_half, second_half], 1).reshape(
        seq_count, 2 * n_ctx * half_rows, model_cols
    )


def to_devices(ordered, pair_of, n_ctx, half_rows):
    seq_count, model_cols = (ordered.shape[0], ordered.shape[2])
    blocks = ordered.reshape(seq_count, 2 * n_ctx, half_rows, model_cols)
    first_slot = jnp.take(blocks, pair_of, axis=1)
    second_slot = jnp.take(blocks, 2 * n_ctx - 1 - pair_of, axis=1)
    return jnp.stack([first_slot, second_slot], 2).reshape(
        seq_count, 2 * n_ctx * half_rows, model_cols
    )


def attend(query_group, first_position, keyval_order, tile_rows, key_width, score_scale):
    seq_count, block_rows, kv_heads, groups, head_size = query_group.shape
    query_pos = first_position + jnp.arange(block_rows, dtype=jnp.int32)
    tile_count = (first_position + block_rows + tile_rows - 1) // tile_rows

    def tile_step(tile_index, carried):
        running_max, running_sum, weighted = carried
        piece = lax.dynamic_slice_in_dim(keyval_order, tile_index * tile_rows, tile_rows, 1)
        keys = piece[..., :key_width].reshape(seq_count, tile_rows, kv_heads, head_size)
        values = piece[..., key_width:].reshape(seq_count, tile_rows, kv_heads, head_size)
        scores = (
            jnp.einsum("sqkgd,stkd->skgqt", query_group, keys, preferred_element_type=jnp.float32)
            * score_scale
        )
        key_pos = tile_index * tile_rows + jnp.arange(tile_rows, dtype=jnp.int32)
        allowed = key_pos[None, :] <= query_pos[:, None]
        scores = jnp.where(allowed, scores, -jnp.inf)
        fresh_max = jnp.maximum(running_max, jnp.max(scores, -1))
        weights = jnp.exp(scores - fresh_max[..., None])
        factor = jnp.exp(running_max - fresh_max)
        running_sum = running_sum * factor + jnp.sum(weights, -1)
        update = jnp.einsum(
            "skgqt,stkd->skgqd",
            weights.astype(jnp.bfloat16),
            values,
            preferred_element_type=jnp.float32,
        )
        weighted = weighted * factor[..., None] + update
        return (fresh_max, running_sum, weighted)

    start_state = (
        jnp.full((seq_count, kv_heads, groups, block_rows), -jnp.inf, jnp.float32),
        jnp.zeros((seq_count, kv_heads, groups, block_rows), jnp.float32),
        jnp.zeros((seq_count, kv_heads, groups, block_rows, head_size), jnp.float32),
    )
    running_max, running_sum, weighted = lax.fori_loop(0, tile_count, tile_step, start_state)
    return (weighted / running_sum[..., None], running_max + jnp.log(running_sum))


def attend_back(
    query_group,
    first_position,
    keyval_order,
    grad_group,
    delta,
    log_total,
    grad_keyval,
    tile_rows,
    key_width,
    score_scale,
):
    seq_count, block_rows, kv_heads, groups, head_size = query_group.shape
    query_pos = first_position + jnp.arange(block_rows, dtype=jnp.int32)
    tile_count = (first_position + block_rows + tile_rows - 1) // tile_rows

    def tile_step(tile_index, carried):
        grad_query, grad_pairs = carried
        piece = lax.dynamic_slice_in_dim(keyval_order, tile_index * tile_rows, tile_rows, 1)
        keys = piece[..., :key_width].reshape(seq_count, tile_rows, kv_heads, head_size)
        values = piece[..., key_width:].reshape(seq_count, tile_rows, kv_heads, head_size)
        scores = (
            jnp.einsum("sqkgd,stkd->skgqt", query_group, keys, preferred_element_type=jnp.float32)
            * score_scale
        )
        key_pos = tile_index * tile_rows + jnp.arange(tile_rows, dtype=jnp.int32)
        allowed = key_pos[None, :] <= query_pos[:, None]
        probs = jnp.exp(jnp.where(allowed, scores, -jnp.inf) - log_total[..., None])
        grad_values = jnp.einsum(
            "skgqt,sqkgd->stkd",
            probs.astype(jnp.bfloat16),
            grad_group,
            preferred_element_type=jnp.float32,
        )
        grad_probs = jnp.einsum(
            "sqkgd,stkd->skgqt", grad_group, values, preferred_element_type=jnp.float32
        )
        grad_scores = (probs * (grad_probs - delta[..., None])).astype(jnp.bfloat16)
        grad_query = (
            grad_query
            + jnp.einsum("skgqt,stkd->sqkgd", grad_scores, keys, preferred_element_type=jnp.float32)
            * score_scale
        )
        grad_keys = (
            jnp.einsum(
                "skgqt,sqkgd->stkd", grad_scores, query_group, preferred_element_type=jnp.float32
            )
            * score_scale
        )
        joined = jnp.concatenate(
            [
                grad_keys.reshape(seq_count, tile_rows, key_width),
                grad_values.reshape(seq_count, tile_rows, key_width),
            ],
            -1,
        )
        previous = lax.dynamic_slice_in_dim(grad_pairs, tile_index * tile_rows, tile_rows, 1)
        grad_pairs = lax.dynamic_update_slice_in_dim(
            grad_pairs, previous + joined, tile_index * tile_rows, 1
        )
        return (grad_query, grad_pairs)

    start_state = (
        jnp.zeros((seq_count, block_rows, kv_heads, groups, head_size), jnp.float32),
        grad_keyval,
    )
    return lax.fori_loop(0, tile_count, tile_step, start_state)


def on_device(
    hidden,
    pair_of,
    attn_gain,
    query_weight,
    query_bias,
    key_weight,
    key_bias,
    value_weight,
    value_bias,
    out_weight,
    mlp_gain,
    gate_weight,
    up_weight,
    down_weight,
    cotangent,
):
    gain_one, query_full, qbias_full, key_full, kbias_full, value_full, vbias_full, out_full = (
        lax.all_gather(attn_gain, "fsdp", axis=0, tiled=True),
        lax.all_gather(query_weight, "fsdp", axis=0, tiled=True),
        lax.all_gather(query_bias, "fsdp", axis=0, tiled=True),
        lax.all_gather(key_weight, "fsdp", axis=0, tiled=True),
        lax.all_gather(key_bias, "fsdp", axis=0, tiled=True),
        lax.all_gather(value_weight, "fsdp", axis=0, tiled=True),
        lax.all_gather(value_bias, "fsdp", axis=0, tiled=True),
        lax.all_gather(out_weight, "fsdp", axis=0, tiled=True),
    )
    gain_two, gate_full, up_full, down_full = (
        lax.all_gather(mlp_gain, "fsdp", axis=0, tiled=True),
        lax.all_gather(gate_weight, "fsdp", axis=0, tiled=True),
        lax.all_gather(up_weight, "fsdp", axis=0, tiled=True),
        lax.all_gather(down_weight, "fsdp", axis=0, tiled=True),
    )
    seq_count, local_rows, model_width = hidden.shape
    half_rows = local_rows // 2
    key_width = key_full.shape[1]
    groups = H // KVH
    score_scale = 1.0 / math.sqrt(HD)
    n_ctx = lax.axis_size("ctx")
    ctx_place = lax.axis_index("ctx")
    devices = jnp.arange(n_ctx, dtype=jnp.int32)
    own_pair = jnp.sum(jnp.where(devices == ctx_place, pair_of, 0))
    holder = jnp.sum(jnp.where(pair_of[None, :] == devices[:, None], devices[None, :], 0), 1)
    starts = [own_pair * half_rows, (2 * n_ctx - 1 - own_pair) * half_rows]
    offsets = jnp.arange(half_rows, dtype=jnp.int32)
    positions = jnp.concatenate([starts[0] + offsets, starts[1] + offsets])
    cosine, sine = rotary_tables(positions)
    inputs = hidden.astype(jnp.float32)
    gain_one32 = gain_one.astype(jnp.float32)
    gain_two32 = gain_two.astype(jnp.float32)
    normed_one, inverse_one = normalize(inputs, gain_one32)
    normed_one = normed_one.astype(jnp.bfloat16)
    queries = rotary(
        project(normed_one, query_full, qbias_full).reshape(seq_count, local_rows, H, HD),
        cosine,
        sine,
    ).astype(jnp.bfloat16)
    keys = rotary(
        project(normed_one, key_full, kbias_full).reshape(seq_count, local_rows, KVH, HD),
        cosine,
        sine,
    ).astype(jnp.bfloat16)
    values = project(normed_one, value_full, vbias_full).astype(jnp.bfloat16)
    keyval_local = jnp.concatenate([keys.reshape(seq_count, local_rows, key_width), values], -1)
    keyval_order = to_sequence(
        lax.all_gather(keyval_local, "ctx", axis=1, tiled=True), holder, n_ctx, half_rows
    )
    tile_rows = math.gcd(1024, keyval_order.shape[1])
    query_groups = queries.reshape(seq_count, local_rows, KVH, groups, HD)
    head_outs = []
    log_totals = []
    for slot_index in range(2):
        head_out, log_total = attend(
            query_groups[:, slot_index * half_rows : (slot_index + 1) * half_rows],
            starts[slot_index],
            keyval_order,
            tile_rows,
            key_width,
            score_scale,
        )
        head_outs.append(head_out)
        log_totals.append(log_total)
    heads = jnp.concatenate(
        [part.transpose(0, 3, 1, 2, 4).reshape(seq_count, half_rows, H * HD) for part in head_outs],
        1,
    ).astype(jnp.bfloat16)
    resid = inputs + jnp.einsum("sre,ed->srd", heads, out_full, preferred_element_type=jnp.float32)
    normed_two, inverse_two = normalize(resid, gain_two32)
    normed_two = normed_two.astype(jnp.bfloat16)
    gate_values = jnp.einsum(
        "srd,df->srf", normed_two, gate_full, preferred_element_type=jnp.float32
    )
    up_values = jnp.einsum("srd,df->srf", normed_two, up_full, preferred_element_type=jnp.float32)
    sigmoid_gate = jax.nn.sigmoid(gate_values)
    silu_gate = gate_values * sigmoid_gate
    activation = (silu_gate * up_values).astype(jnp.bfloat16)
    output = (
        resid + jnp.einsum("srf,fd->srd", activation, down_full, preferred_element_type=jnp.float32)
    ).astype(jnp.bfloat16)
    down_grad = jnp.einsum("srf,srd->fd", activation, cotangent, preferred_element_type=jnp.float32)
    grad_act = jnp.einsum("srd,fd->srf", cotangent, down_full, preferred_element_type=jnp.float32)
    grad_gate = (
        grad_act * up_values * sigmoid_gate * (1.0 + gate_values * (1.0 - sigmoid_gate))
    ).astype(jnp.bfloat16)
    grad_up = (grad_act * silu_gate).astype(jnp.bfloat16)
    gate_grad = jnp.einsum("srd,srf->df", normed_two, grad_gate, preferred_element_type=jnp.float32)
    up_grad = jnp.einsum("srd,srf->df", normed_two, grad_up, preferred_element_type=jnp.float32)
    grad_two = jnp.einsum(
        "srf,df->srd", grad_gate, gate_full, preferred_element_type=jnp.float32
    ) + jnp.einsum("srf,df->srd", grad_up, up_full, preferred_element_type=jnp.float32)
    grad_norm_two, gain_two_grad = norm_back(resid, inverse_two, gain_two32, grad_two)
    grad_resid = cotangent.astype(jnp.float32) + grad_norm_two
    grad_attn = grad_resid.astype(jnp.bfloat16)
    out_grad = jnp.einsum("sre,srd->ed", heads, grad_attn, preferred_element_type=jnp.float32)
    grad_heads = jnp.einsum(
        "srd,ed->sre", grad_attn, out_full, preferred_element_type=jnp.float32
    ).astype(jnp.bfloat16)
    grad_groups = grad_heads.reshape(seq_count, local_rows, KVH, groups, HD)
    grad_keyval = jnp.zeros((seq_count, keyval_order.shape[1], 2 * key_width), jnp.float32)
    grad_query_parts = []
    for slot_index in range(2):
        grad_slot = grad_groups[:, slot_index * half_rows : (slot_index + 1) * half_rows]
        delta = jnp.einsum(
            "sqkgd,skgqd->skgq", grad_slot.astype(jnp.float32), head_outs[slot_index]
        )
        grad_query, grad_keyval = attend_back(
            query_groups[:, slot_index * half_rows : (slot_index + 1) * half_rows],
            starts[slot_index],
            keyval_order,
            grad_slot,
            delta,
            log_totals[slot_index],
            grad_keyval,
            tile_rows,
            key_width,
            score_scale,
        )
        grad_query_parts.append(grad_query)
    grad_query_rot = jnp.concatenate(grad_query_parts, 1).reshape(seq_count, local_rows, H, HD)
    own_pairs = lax.psum_scatter(
        to_devices(grad_keyval, pair_of, n_ctx, half_rows), "ctx", scatter_dimension=1, tiled=True
    )
    grad_key_rot = own_pairs[..., :key_width].reshape(seq_count, local_rows, KVH, HD)
    grad_value = own_pairs[..., key_width:].astype(jnp.bfloat16)
    grad_query_pre = (
        rotary_back(grad_query_rot, cosine, sine)
        .reshape(seq_count, local_rows, H * HD)
        .astype(jnp.bfloat16)
    )
    grad_key_pre = (
        rotary_back(grad_key_rot, cosine, sine)
        .reshape(seq_count, local_rows, key_width)
        .astype(jnp.bfloat16)
    )
    query_grad = jnp.einsum(
        "srd,sre->de", normed_one, grad_query_pre, preferred_element_type=jnp.float32
    )
    key_grad = jnp.einsum(
        "srd,sre->de", normed_one, grad_key_pre, preferred_element_type=jnp.float32
    )
    value_grad = jnp.einsum(
        "srd,sre->de", normed_one, grad_value, preferred_element_type=jnp.float32
    )
    qbias_grad = jnp.sum(grad_query_pre.astype(jnp.float32), (0, 1))
    kbias_grad = jnp.sum(grad_key_pre.astype(jnp.float32), (0, 1))
    vbias_grad = jnp.sum(grad_value.astype(jnp.float32), (0, 1))
    grad_one = (
        jnp.einsum("sre,de->srd", grad_query_pre, query_full, preferred_element_type=jnp.float32)
        + jnp.einsum("sre,de->srd", grad_key_pre, key_full, preferred_element_type=jnp.float32)
        + jnp.einsum("sre,de->srd", grad_value, value_full, preferred_element_type=jnp.float32)
    )
    grad_norm_one, gain_one_grad = norm_back(inputs, inverse_one, gain_one32, grad_one)
    input_grad = (grad_resid + grad_norm_one).astype(jnp.bfloat16)
    (
        gain_one_part,
        query_part,
        qbias_part,
        key_part,
        kbias_part,
        value_part,
        vbias_part,
        out_part,
        gain_two_part,
        gate_part,
        up_part,
        down_part,
    ) = (
        lax.psum_scatter(
            gain_one_grad.astype(jnp.bfloat16), "fsdp", scatter_dimension=0, tiled=True
        ).astype(jnp.float32),
        lax.psum_scatter(
            query_grad.astype(jnp.bfloat16), "fsdp", scatter_dimension=0, tiled=True
        ).astype(jnp.float32),
        lax.psum_scatter(
            qbias_grad.astype(jnp.bfloat16), "fsdp", scatter_dimension=0, tiled=True
        ).astype(jnp.float32),
        lax.psum_scatter(
            key_grad.astype(jnp.bfloat16), "fsdp", scatter_dimension=0, tiled=True
        ).astype(jnp.float32),
        lax.psum_scatter(
            kbias_grad.astype(jnp.bfloat16), "fsdp", scatter_dimension=0, tiled=True
        ).astype(jnp.float32),
        lax.psum_scatter(
            value_grad.astype(jnp.bfloat16), "fsdp", scatter_dimension=0, tiled=True
        ).astype(jnp.float32),
        lax.psum_scatter(
            vbias_grad.astype(jnp.bfloat16), "fsdp", scatter_dimension=0, tiled=True
        ).astype(jnp.float32),
        lax.psum_scatter(
            out_grad.astype(jnp.bfloat16), "fsdp", scatter_dimension=0, tiled=True
        ).astype(jnp.float32),
        lax.psum_scatter(
            gain_two_grad.astype(jnp.bfloat16), "fsdp", scatter_dimension=0, tiled=True
        ).astype(jnp.float32),
        lax.psum_scatter(
            gate_grad.astype(jnp.bfloat16), "fsdp", scatter_dimension=0, tiled=True
        ).astype(jnp.float32),
        lax.psum_scatter(
            up_grad.astype(jnp.bfloat16), "fsdp", scatter_dimension=0, tiled=True
        ).astype(jnp.float32),
        lax.psum_scatter(
            down_grad.astype(jnp.bfloat16), "fsdp", scatter_dimension=0, tiled=True
        ).astype(jnp.float32),
    )
    (
        gain_one_total,
        query_total,
        qbias_total,
        key_total,
        kbias_total,
        value_total,
        vbias_total,
        out_total,
        gain_two_total,
        gate_total,
        up_total,
        down_total,
    ) = lax.psum(
        (
            gain_one_part,
            query_part,
            qbias_part,
            key_part,
            kbias_part,
            value_part,
            vbias_part,
            out_part,
            gain_two_part,
            gate_part,
            up_part,
            down_part,
        ),
        "ctx",
    )
    return (
        output,
        input_grad,
        gain_one_total,
        query_total,
        qbias_total,
        key_total,
        kbias_total,
        value_total,
        vbias_total,
        out_total,
        gain_two_total,
        gate_total,
        up_total,
        down_total,
    )


def solution(mesh):
    in_specs = (
        P("fsdp", "ctx", None),
        P(),
        P("fsdp"),
        P("fsdp", None),
        P("fsdp"),
        P("fsdp", None),
        P("fsdp"),
        P("fsdp", None),
        P("fsdp"),
        P("fsdp", None),
        P("fsdp"),
        P("fsdp", None),
        P("fsdp", None),
        P("fsdp", None),
        P("fsdp", "ctx", None),
    )
    out_specs = (
        P("fsdp", "ctx", None),
        P("fsdp", "ctx", None),
        P("fsdp"),
        P("fsdp", None),
        P("fsdp"),
        P("fsdp", None),
        P("fsdp"),
        P("fsdp", None),
        P("fsdp"),
        P("fsdp", None),
        P("fsdp"),
        P("fsdp", None),
        P("fsdp", None),
        P("fsdp", None),
    )
    return jax.shard_map(
        on_device, mesh=mesh, in_specs=in_specs, out_specs=out_specs, check_vma=False
    )
```

profile of v0, /device:TPU:20, one launch (start us, length us, event | category | flops | bytes accessed | tf_op | source)
XLA Modules:
  0.0 1595.3 jit_solution(2118416334528541037)
XLA Ops:
  8.0 1.3 fusion.174
  10.6 1.3 compare_select_fusion.1
  17.5 5.2 all-reduce.12
  22.8 8.7 all_gather.40
  31.7 1.1 fusion.124
  33.3 1.3 convolution_add_fusion.5
  34.6 8.2 all_gather.42
  43.6 1.3 fusion.121
  49.6 1.9 convolution_add_fusion.2
  52.3 29.7 %all-gather.7.cloned.1.call-done = bf16[1,2048,256]{1,2,0:T(8,128)(2,1)} async-done(((bf16[1,128,256]{1,2,0:T(8,128)(2,1)}), bf16[1,2048,256]{1,2,0:T(8,128)(2,1)}) %all-gather.7.cloned.1.call-update) | async-done | bytes 1048592 | tf_op jit(solution)/shard_map/all_gather | solution.py:255
  82.0 1.5 copy.106
  84.4 1.6 gather_fusion
  87.6 1.1 pad_maximum_fusion.1
  89.5 3.0 while.56
  91.4 1.1 fusion.269
  93.1 6.2 while.57
  95.0 1.1 fusion.276
  98.0 1.1 fusion.276
  99.9 11.4 all-gather.11.cloned.1.call-done
  111.4 1.9 multiply_reduce_fusion
  113.5 109.4 %all-gather.15.cloned.1.call-done = bf16[896,4864]{1,0:T(8,128)(2,1)} async-done(((bf16[448,4864]{1,0:T(8,128)(2,1)}), bf16[896,4864]{1,0:T(8,128)(2,1)}) %all-gather.15.cloned.1.call-update) | async-done | bytes 8716304 | tf_op jit(solution)/shard_map/all_gather | solution.py:220
  222.9 6.4 fusion.176
  229.3 105.1 %all-gather.13.cloned.1.call-done = bf16[896,4864]{1,0:T(8,128)(2,1)} async-done(((bf16[448,4864]{1,0:T(8,128)(2,1)}), bf16[896,4864]{1,0:T(8,128)(2,1)}) %all-gather.13.cloned.1.call-update) | async-done | bytes 8716304 | tf_op jit(solution)/shard_map/all_gather | solution.py:219
  334.4 6.4 fusion.175
  340.8 105.1 %all-gather.17.cloned.1.call-done = bf16[4864,896]{1,0:T(8,128)(2,1)} async-done(((bf16[2432,896]{1,0:T(8,128)(2,1)}), bf16[4864,896]{1,0:T(8,128)(2,1)}) %all-gather.17.cloned.1.call-update) | async-done | bytes 8716304 | tf_op jit(solution)/shard_map/all_gather | solution.py:221
  446.0 8.7 multiply_convert_fusion
  454.6 2.8 fusion.177
  457.5 6.5 fusion.138
  466.6 1.0 copy.148
  467.6 1.4 fusion.140
  470.6 6.1 while.58
  471.0 1.6 fusion.287
  472.6 1.0 fusion.290
  473.7 1.3 fusion.288
  477.5 10.0 while.59
  478.5 1.0 fusion.306
  479.5 1.3 fusion.304
  483.5 1.0 fusion.306
  484.5 1.3 fusion.304
  487.5 1.8 copy.118
  489.3 2.3 gather_fusion.3
  491.7 2.3 gather_fusion.2
  494.6 1.5 copy.119
  496.1 1.8 convolution_convert_fusion.3
  499.2 1.8 convolution_convert_fusion.4
  501.8 55.1 %reduce-scatter.9.cloned.1.call-done = f32[1,128,256]{2,1,0:T(8,128)} async-done(((f32[1,2048,256]{2,1,0:T(8,128)}), f32[1,128,256]{2,1,0:T(8,128)}) %reduce-scatter.9.cloned.1.call-update) | async-done | bytes 131088 | tf_op jit(solution)/shard_map/reduce_scatter | solution.py:329
  558.0 1.9 convolution_convert_fusion.6
  560.0 1.5 fusion.170
  561.4 1.0 convolution_convert_fusion.7
  562.8 5.8 convolution_convert_fusion
  569.5 7.3 convolution_convert_fusion.1
  576.9 7.3 convolution_convert_fusion.2
  585.5 1.3 fusion.151
  586.9 1.1 fusion.139
  588.0 2.0 fusion.178
  590.2 5.8 fusion.119
  596.6 5.3 all-reduce.11
  603.1 12.7 reduce-scatter.11.cloned.1.call-done
  615.9 13.5 reduce-scatter.15.cloned.1.call-done
  629.3 14.3 reduce-scatter.13.cloned.1.call-done
  643.6 105.6 %reduce-scatter.23.cloned.1.call-done = bf16[2432,896]{1,0:T(8,128)(2,1)} async-done(((bf16[4864,896]{1,0:T(8,128)(2,1)}), bf16[2432,896]{1,0:T(8,128)(2,1)}) %reduce-scatter.23.cloned.1.call-update) | async-done | bytes 4358160 | tf_op jit(solution)/shard_map/reduce_scatter | solution.py:410
  749.3 105.8 %reduce-scatter.21.cloned.1.call-done = bf16[448,4864]{1,0:T(8,128)(2,1)} async-done(((bf16[896,4864]{1,0:T(8,128)(2,1)}), bf16[448,4864]{1,0:T(8,128)(2,1)}) %reduce-scatter.21.cloned.1.call-update) | async-done | bytes 4358160 | tf_op jit(solution)/shard_map/reduce_scatter | solution.py:407
  855.0 105.6 %reduce-scatter.19.cloned.1.call-done = bf16[448,4864]{1,0:T(8,128)(2,1)} async-done(((bf16[896,4864]{1,0:T(8,128)(2,1)}), bf16[448,4864]{1,0:T(8,128)(2,1)}) %reduce-scatter.19.cloned.1.call-update) | async-done | bytes 4358160 | tf_op jit(solution)/shard_map/reduce_scatter | solution.py:404
  960.7 627.6 %all-reduce.14 = (f32[448]{0:T(512)}, f32[448,896]{1,0:T(8,128)}, f32[448]{0:T(512)}, f32[448,128]{1,0:T(8,128)}, f32[64]{0:T(128)}, /*index=5*/f32[448,128]{1,0...) all-reduce(f32[448]{0:T(512)S(1)} %dynamic-slice_convert_fusion.2, ...), channel_id=1, replica_groups=mesh['ctx'=16,'fsdp'=2] {'ctx'}, use_global_device_ids=true, to_apply=%region_21.24 | all-reduce | flops 7456192 | bytes 44740096 | tf_op jit(solution)/shard_map/psum | solution.py:427
  (282 shorter events, 40.9 us)
Async XLA Ops:
  7.2 42.4 %all-gather.9.cloned.1.call-start = ((), (), s32[]{:S(2)}) async-start(), calls=%async_computation.9 | async-start | bytes 2408448 | tf_op jit(solution)/shard_map/all_gather | solution.py:209
  7.9 74.1 %all-gather.7.cloned.1.call-start = ((), (), s32[]{:S(2)}) async-start(), calls=%async_computation.8 | async-start | bytes 1114112 | tf_op jit(solution)/shard_map/all_gather | solution.py:255
  22.7 26.8 %copy-start.39 = (f32[896]{0:T(1024)}, f32[896]{0:T(1024)S(1)}, u32[]{:S(2)}) copy-start(f32[896]{0:T(1024)S(1)} %convert_element_type.219) | copy-start | bytes 10756
  31.5 1.8 copy-start.28
  31.7 20.0 %copy-start.23 = (f32[128,64]{0,1:T(8,128)}, f32[128,64]{0,1:T(8,128)S(1)}, u32[]{:S(2)}) copy-start(f32[128,64]{0,1:T(8,128)S(1)} %get-tuple-element.612) | copy-start | bytes 98308
  31.7 20.0 %copy-start.32 = (f32[128,64]{0,1:T(8,128)}, f32[128,64]{0,1:T(8,128)S(1)}, u32[]{:S(2)}) copy-start(f32[128,64]{0,1:T(8,128)S(1)} %get-tuple-element.613) | copy-start | bytes 98308
  33.3 16.2 %copy-start.41 = (f32[128]{0:T(128)}, f32[128]{0:T(128)S(1)}, u32[]{:S(2)}) copy-start(f32[128]{0:T(128)S(1)} %get-tuple-element.617) | copy-start | bytes 1540
  45.5 65.9 %all-gather.11.cloned.1.call-start = ((), (), s32[]{:S(2)}) async-start(), calls=%async_computation.10 | async-start | bytes 2408448 | tf_op jit(solution)/shard_map/all_gather | solution.py:215
  46.2 176.7 %all-gather.15.cloned.1.call-start = ((), (), s32[]{:S(2)}) async-start(), calls=%async_computation.12 | async-start | bytes 13074432 | tf_op jit(solution)/shard_map/all_gather | solution.py:220
  46.8 1.2 copy-start.47
  46.8 2.7 copy-start.9
  46.8 287.6 %all-gather.13.cloned.1.call-start = ((), (), s32[]{:S(2)}) async-start(), calls=%async_computation.11 | async-start | bytes 13074432 | tf_op jit(solution)/shard_map/all_gather | solution.py:219
  47.4 398.5 %all-gather.17.cloned.1.call-start = ((), (), s32[]{:S(2)}) async-start(), calls=%async_computation.13 | async-start | bytes 13074432 | tf_op jit(solution)/shard_map/all_gather | solution.py:221
  48.0 508.9 %reduce-scatter.9.cloned.1.call-start = ((), (), s32[]{:S(2)}) async-start(), calls=%async_computation.14 | async-start | bytes 2228224 | tf_op jit(solution)/shard_map/reduce_scatter | solution.py:329
  52.0 35.5 %copy-start.1 = (bf16[1,64,2,7,64]{1,4,3,2,0:T(8,128)(2,1)}, bf16[1,64,2,7,64]{1,4,3,2,0:T(8,128)(2,1)S(1)}, u32[]{:S(2)}) copy-start(bf16[1,64,2,7,64]{1,4,3,2,0:T(8,128)(2,1)S(1)} %get-tuple-element.972) | copy-start | bytes 344068
  99.9 129.4 %copy-start.25 = (bf16[128,896]{1,0:T(8,128)(2,1)}, bf16[128,896]{1,0:T(8,128)(2,1)S(1)}, u32[]{:S(2)}) copy-start(bf16[128,896]{1,0:T(8,128)(2,1)S(1)} %constant_dynamic-update-slice_fusion) | copy-start | bytes 688132
  113.3 350.7 %copy-start.12 = (f32[1,128,896]{2,1,0:T(8,128)}, f32[1,128,896]{2,1,0:T(8,128)S(1)}, u32[]{:S(2)}) copy-start(f32[1,128,896]{2,1,0:T(8,128)S(1)} %get-tuple-element.624) | copy-start | bytes 1376260
  113.5 221.0 %copy-start.14 = (bf16[128,896]{1,0:T(8,128)(2,1)}, bf16[128,896]{1,0:T(8,128)(2,1)S(1)}, u32[]{:S(2)}) copy-start(bf16[128,896]{1,0:T(8,128)(2,1)S(1)} %fusion.144) | copy-start | bytes 688132
  229.3 216.6 %copy-start.27 = (bf16[1,128,896]{2,1,0:T(8,128)(2,1)S(1)}, bf16[1,128,896]{2,1,0:T(8,128)(2,1)}, u32[]{:S(2)}) copy-start(bf16[1,128,896]{2,1,0:T(8,128)(2,1)} %param.41) | copy-start | bytes 688132
  446.0 8.7 copy-start
  454.6 2.8 copy-start.20
  454.6 2.8 copy-start.21
  457.4 7.5 copy-start.19
  464.2 0.8 copy-start.16
  470.8 1.8 copy-start.38
  473.6 1.4 copy-start.6
  473.7 2.3 copy-start.2
  475.9 0.8 copy-start.7
  477.5 0.9 copy-start.37
  479.5 1.4 copy-start.3
  481.7 0.8 copy-start.4
  482.5 0.9 copy-start.37
  484.5 1.3 copy-start.3
  487.5 6.5 copy-start.46
  489.3 4.8 copy-start.45
  494.5 1.6 copy-start.17
  494.5 1.6 copy-start.26
  496.0 2.0 copy-start.5
  496.0 2.0 copy-start.8
  496.0 2.2 copy-start.33
  496.0 2.2 copy-start.24
  496.1 107.1 %reduce-scatter.17.cloned.1.call-start = ((), (), s32[]{:S(2)}) async-start(), calls=%async_computation.18 | async-start | bytes 2408448 | tf_op jit(solution)/shard_map/reduce_scatter | solution.py:398
  497.9 1.3 copy-start.10
  497.9 1.3 copy-start.40
  497.9 1.3 copy-start.42
  497.9 117.9 %reduce-scatter.11.cloned.1.call-start = ((), (), s32[]{:S(2)}) async-start(), calls=%async_computation.15 | async-start | bytes 2408448 | tf_op jit(solution)/shard_map/reduce_scatter | solution.py:380
  498.3 63.2 %copy-start.22 = (f32[1,128,14,32]{1,3,2,0:T(8,128)}, f32[1,128,14,32]{1,3,2,0:T(8,128)S(1)}, u32[]{:S(2)}) copy-start(f32[1,128,14,32]{1,3,2,0:T(8,128)S(1)} %get-tuple-element.598) | copy-start | bytes 688132
  498.3 64.5 %copy-start.11 = (bf16[128,4864]{1,0:T(8,128)(2,1)S(1)}, bf16[128,4864]{1,0:T(8,128)(2,1)}, u32[]{:S(2)}) copy-start(bf16[128,4864]{1,0:T(8,128)(2,1)} %get-tuple-element.592) | copy-start | bytes 3735556
  501.1 128.3 %reduce-scatter.15.cloned.1.call-start = ((), (), s32[]{:S(2)}) async-start(), calls=%async_computation.17 | async-start | bytes 344064 | tf_op jit(solution)/shard_map/reduce_scatter | solution.py:392
  559.9 83.7 %reduce-scatter.13.cloned.1.call-start = ((), (), s32[]{:S(2)}) async-start(), calls=%async_computation.16 | async-start | bytes 344064 | tf_op jit(solution)/shard_map/reduce_scatter | solution.py:386
  561.4 7.2 copy-start.35
  562.5 186.8 %reduce-scatter.23.cloned.1.call-start = ((), (), s32[]{:S(2)}) async-start(), calls=%async_computation.21 | async-start | bytes 13074432 | tf_op jit(solution)/shard_map/reduce_scatter | solution.py:410
  568.6 0.9 copy-start.15
  568.6 286.4 %reduce-scatter.21.cloned.1.call-start = ((), (), s32[]{:S(2)}) async-start(), calls=%async_computation.20 | async-start | bytes 13074432 | tf_op jit(solution)/shard_map/reduce_scatter | solution.py:407
  576.8 383.9 %reduce-scatter.19.cloned.1.call-start = ((), (), s32[]{:S(2)}) async-start(), calls=%async_computation.19 | async-start | bytes 13074432 | tf_op jit(solution)/shard_map/reduce_scatter | solution.py:404
  584.2 5.9 copy-start.13
  590.1 5.8 copy-start.29
  590.1 5.8 copy-start.36
  590.1 6.1 copy-start.31
  590.1 6.1 copy-start.34
  590.1 6.4 copy-start.43
  590.1 6.4 copy-start.44
  590.1 12.1 copy-start.18
  590.1 12.1 copy-start.48
  (2 other events, 1.5 us)
Sparse Core Ops, SparseCore 0:
  9.5 33.6 all-gather.8
  45.9 36.0 all-gather.6
  83.6 27.7 all-gather.10
  112.8 110.1 all-gather.14
  224.3 110.0 all-gather.12
  335.9 110.0 all-gather.16
  496.2 60.7 reduce-scatter.8
  559.8 26.4 reduce-scatter.16
  589.1 26.6 reduce-scatter.10
  617.9 11.3 reduce-scatter.14
  632.2 11.3 reduce-scatter.12
  646.4 102.8 reduce-scatter.22
  752.1 102.8 reduce-scatter.20
  857.8 102.8 reduce-scatter.18
where the time goes:
time: 1600 us
  waiting for transfers between devices  777 us (49%)
  blocking collectives  655 us (41%)
  matrix products  92.5 us (6%)
  local copies, waits for them, and re-layouts  28.3 us (2%)
  other arithmetic  21.8 us (1%)
  between operations  19.3 us (1%)
    psum x1, blocking collectives, on_device(): lax.psum((gain_one_part, query_part, qbias_part, key_part, kbias_part, va...  628 us
    all_gather x1, waiting for transfers between devices, on_device(): lax.all_gather(up_weight, 'fsdp', axis=0, tiled=True)  109 us
    reduce_scatter x1, waiting for transfers between devices, on_device(): lax.psum_scatter(up_grad.astype(jnp.bfloat16), 'fsdp', scatter_dimension=...  106 us
    reduce_scatter x1, waiting for transfers between devices, on_device(): lax.psum_scatter(down_grad.astype(jnp.bfloat16), 'fsdp', scatter_dimensio...  106 us
    reduce_scatter x1, waiting for transfers between devices, on_device(): lax.psum_scatter(gate_grad.astype(jnp.bfloat16), 'fsdp', scatter_dimensio...  106 us
    all_gather x1, waiting for transfers between devices, on_device(): lax.all_gather(down_weight, 'fsdp', axis=0, tiled=True)  105 us
    all_gather x1, waiting for transfers between devices, on_device(): lax.all_gather(gate_weight, 'fsdp', axis=0, tiled=True)  105 us
    reduce_scatter x1, waiting for transfers between devices, on_device(): lax.psum_scatter(to_devices(grad_keyval, pair_of, n_ctx, half_rows), 'ctx...  55.1 us
  transfers between devices with their start and end apart: 14, of which 12 were waited for; matrix products, arithmetic and copies ran while one was open for 6% of the time, Pallas kernels for 0%

commit v1 on v0

v1 whole, which is shorter than its diff:
```python
import math

import jax
import jax.numpy as jnp
from jax import lax
from jax.sharding import PartitionSpec as P

H = 14
KVH = 2
HD = 64

EPSILON = 1e-06
THETA_BASE = 1000000.0

BF16 = jnp.bfloat16
F32 = jnp.float32


def rotate_half(values):
    middle = values.shape[-1] // 2
    return jnp.concatenate([-values[..., middle:], values[..., :middle]], -1)


def rotate_back(values):
    middle = values.shape[-1] // 2
    return jnp.concatenate([values[..., middle:], -values[..., :middle]], -1)


def rotary(values, cosine, sine):
    return values * cosine + rotate_half(values) * sine


def rotary_back(values, cosine, sine):
    return values * cosine + rotate_back(values * sine)


def rotary_tables(positions):
    middle = HD // 2
    freqs = jnp.power(THETA_BASE, -2.0 * jnp.arange(middle, dtype=F32) / HD)
    angle = positions.astype(F32)[:, None] * freqs[None, :]
    angle = jnp.concatenate([angle, angle], -1)[:, None, :]
    return (jnp.cos(angle), jnp.sin(angle))


def normalize(values, gain):
    inverse = lax.rsqrt(jnp.mean(values * values, -1, keepdims=True) + EPSILON)
    return (values * inverse * gain, inverse)


def norm_back(values, inverse, gain, grad):
    scaled = gain * grad
    mean_term = jnp.mean(scaled * values, -1, keepdims=True)
    return inverse * scaled - values * inverse**3 * mean_term


def dot(left, right, left_dim=1, right_dim=0):
    return lax.dot_general(
        left, right, (((left_dim,), (right_dim,)), ((), ())), preferred_element_type=F32
    )


class Ring:
    def __init__(self, n_ctx):
        self.chips = n_ctx // 2
        evens = list(range(0, self.chips, 2))
        odds = list(range(1, self.chips, 2))
        self.order = evens + odds[::-1]
        count = self.chips
        self.up = [
            (2 * self.order[i] + core, 2 * self.order[(i + 1) % count] + core)
            for i in range(count)
            for core in range(2)
        ]
        self.down = [(b, a) for a, b in self.up]
        self.swap = [(i, i ^ 1) for i in range(n_ctx)]
        me = lax.axis_index("ctx")
        self.core = me % 2
        chip = me // 2
        self.place = jnp.where(chip % 2 == 0, chip // 2, count - 1 - chip // 2)
        self.offsets = [0]
        for step in range(1, count // 2):
            self.offsets += [-step, step]
        self.offsets.append(count // 2)
        places = (self.place + jnp.array(self.offsets, jnp.int32)) % count
        chips = jnp.where(places < (count + 1) // 2, 2 * places, 2 * (count - 1 - places) + 1)
        self.places = places
        self.own_devices = 2 * chips + self.core
        self.other_devices = 2 * chips + 1 - self.core

    def send_up(self, block):
        return lax.ppermute(block, "ctx", self.up)

    def send_down(self, block):
        return lax.ppermute(block, "ctx", self.down)

    def swap_core(self, block):
        return lax.ppermute(block, "ctx", self.swap)

    def gather(self, block):
        half = block.shape[0] // 2
        steps = self.chips // 2
        blocks = [block]
        low = high = block
        for _ in range(steps - 1):
            low = self.send_up(low)
            high = self.send_down(high)
            blocks += [low, high]
        far = jnp.concatenate([self.send_up(low[:half]), self.send_down(high[half:])], 0)
        return blocks + [far]

    def gather_all(self, block):
        own = self.gather(block)
        other = [self.swap_core(part) for part in own]
        return own + other

    def add(self, left, right):
        return (left.astype(F32) + right.astype(F32)).astype(BF16)

    def scatter(self, blocks):
        steps = self.chips // 2
        half = blocks[0].shape[0] // 2
        at = dict(zip(self.offsets, blocks))
        far = at[steps]
        low = self.send_up(far[:half])
        high = self.send_down(far[half:])
        for step in range(steps - 1, 0, -1):
            ahead, behind = at[step], at[-step]
            if step == steps - 1:
                ahead = jnp.concatenate([self.add(ahead[:half], low), ahead[half:]], 0)
                behind = jnp.concatenate([behind[:half], self.add(behind[half:], high)], 0)
            else:
                ahead = self.add(ahead, low)
                behind = self.add(behind, high)
            low = self.send_up(ahead)
            high = self.send_down(behind)
        return at[0].astype(F32) + low.astype(F32) + high.astype(F32)

    def scatter_all(self, partial):
        count = self.chips
        received = self.swap_core(partial[count:])
        mine = self.add(partial[:count], received)
        return self.scatter([mine[i] for i in range(count)])


def attend(query_group, first_position, keyval_order, tile_rows, key_width, score_scale):
    seq_count, block_rows, kv_heads, groups, head_size = query_group.shape
    query_pos = first_position + jnp.arange(block_rows, dtype=jnp.int32)
    tile_count = (first_position + block_rows + tile_rows - 1) // tile_rows

    def tile_step(tile_index, carried):
        running_max, running_sum, weighted = carried
        piece = lax.dynamic_slice_in_dim(keyval_order, tile_index * tile_rows, tile_rows, 1)
        keys = piece[..., :key_width].reshape(seq_count, tile_rows, kv_heads, head_size)
        values = piece[..., key_width:].reshape(seq_count, tile_rows, kv_heads, head_size)
        scores = (
            jnp.einsum("sqkgd,stkd->skgqt", query_group, keys, preferred_element_type=F32)
            * score_scale
        )
        key_pos = tile_index * tile_rows + jnp.arange(tile_rows, dtype=jnp.int32)
        allowed = key_pos[None, :] <= query_pos[:, None]
        scores = jnp.where(allowed, scores, -jnp.inf)
        fresh_max = jnp.maximum(running_max, jnp.max(scores, -1))
        weights = jnp.exp(scores - fresh_max[..., None])
        factor = jnp.exp(running_max - fresh_max)
        running_sum = running_sum * factor + jnp.sum(weights, -1)
        update = jnp.einsum(
            "skgqt,stkd->skgqd", weights.astype(BF16), values, preferred_element_type=F32
        )
        weighted = weighted * factor[..., None] + update
        return (fresh_max, running_sum, weighted)

    start_state = (
        jnp.full((seq_count, kv_heads, groups, block_rows), -jnp.inf, F32),
        jnp.zeros((seq_count, kv_heads, groups, block_rows), F32),
        jnp.zeros((seq_count, kv_heads, groups, block_rows, head_size), F32),
    )
    running_max, running_sum, weighted = lax.fori_loop(0, tile_count, tile_step, start_state)
    return (weighted / running_sum[..., None], running_max + jnp.log(running_sum))


def attend_back(
    query_group,
    first_position,
    keyval_order,
    grad_group,
    delta,
    log_total,
    grad_keyval,
    tile_rows,
    key_width,
    score_scale,
):
    seq_count, block_rows, kv_heads, groups, head_size = query_group.shape
    query_pos = first_position + jnp.arange(block_rows, dtype=jnp.int32)
    tile_count = (first_position + block_rows + tile_rows - 1) // tile_rows

    def tile_step(tile_index, carried):
        grad_query, grad_pairs = carried
        piece = lax.dynamic_slice_in_dim(keyval_order, tile_index * tile_rows, tile_rows, 1)
        keys = piece[..., :key_width].reshape(seq_count, tile_rows, kv_heads, head_size)
        values = piece[..., key_width:].reshape(seq_count, tile_rows, kv_heads, head_size)
        scores = (
            jnp.einsum("sqkgd,stkd->skgqt", query_group, keys, preferred_element_type=F32)
            * score_scale
        )
        key_pos = tile_index * tile_rows + jnp.arange(tile_rows, dtype=jnp.int32)
        allowed = key_pos[None, :] <= query_pos[:, None]
        probs = jnp.exp(jnp.where(allowed, scores, -jnp.inf) - log_total[..., None])
        grad_values = jnp.einsum(
            "skgqt,sqkgd->stkd", probs.astype(BF16), grad_group, preferred_element_type=F32
        )
        grad_probs = jnp.einsum("sqkgd,stkd->skgqt", grad_group, values, preferred_element_type=F32)
        grad_scores = (probs * (grad_probs - delta[..., None])).astype(BF16)
        grad_query = (
            grad_query
            + jnp.einsum("skgqt,stkd->sqkgd", grad_scores, keys, preferred_element_type=F32)
            * score_scale
        )
        grad_keys = (
            jnp.einsum("skgqt,sqkgd->stkd", grad_scores, query_group, preferred_element_type=F32)
            * score_scale
        )
        joined = jnp.concatenate(
            [
                grad_keys.reshape(seq_count, tile_rows, key_width),
                grad_values.reshape(seq_count, tile_rows, key_width),
            ],
            -1,
        )
        previous = lax.dynamic_slice_in_dim(grad_pairs, tile_index * tile_rows, tile_rows, 1)
        grad_pairs = lax.dynamic_update_slice_in_dim(
            grad_pairs, previous + joined, tile_index * tile_rows, 1
        )
        return (grad_query, grad_pairs)

    start_state = (
        jnp.zeros((seq_count, block_rows, kv_heads, groups, head_size), F32),
        grad_keyval,
    )
    return lax.fori_loop(0, tile_count, tile_step, start_state)


def on_device(
    hidden,
    pair_of,
    attn_gain,
    query_weight,
    query_bias,
    key_weight,
    key_bias,
    value_weight,
    value_bias,
    out_weight,
    mlp_gain,
    gate_weight,
    up_weight,
    down_weight,
    cotangent,
):
    n_ctx = lax.axis_size("ctx")
    ring = Ring(n_ctx)
    chips = n_ctx // 2
    place = lax.axis_index("ctx")
    side = lax.axis_index("fsdp")
    core = ring.core
    flip = [(0, 1), (1, 0)]

    def swap_side(value):
        return lax.ppermute(value, "fsdp", flip)

    def by_side(own, other, axis=0):
        return jnp.where(
            side == 0,
            jnp.concatenate([own, other], axis),
            jnp.concatenate([other, own], axis),
        )

    local_rows, model_width = hidden.shape[1:]
    half_rows = local_rows // 2
    half_width = model_width // 2
    key_width = key_weight.shape[1]
    groups = H // KVH
    score_scale = 1.0 / math.sqrt(HD)
    ffn_half = down_weight.shape[0] // n_ctx
    ffn_cols = 2 * ffn_half

    hidden_own = hidden[0]
    grad_own = cotangent[0]

    small_sizes = (half_width, half_width, half_width, key_width // 2, key_width // 2)
    small_own = jnp.concatenate([attn_gain, mlp_gain, query_bias, key_bias, value_bias])
    small_other = swap_side(small_own)
    smalls = []
    start = 0
    for size in small_sizes:
        smalls.append(by_side(small_own[start : start + size], small_other[start : start + size]))
        start += size
    gain_one, gain_two, qbias, kbias, vbias = [value.astype(F32) for value in smalls]

    attn_own = jnp.concatenate([query_weight, key_weight, value_weight, out_weight], 1)
    quarter = half_width // 2
    attn_piece = swap_side(lax.dynamic_slice_in_dim(attn_own, core * quarter, quarter, 0))
    attn_rest = ring.swap_core(attn_piece)
    attn_other = jnp.where(
        core == 0,
        jnp.concatenate([attn_piece, attn_rest], 0),
        jnp.concatenate([attn_rest, attn_piece], 0),
    )
    attn_full = by_side(attn_own, attn_other)
    query_full = attn_full[:, :model_width]
    keyval_full = attn_full[:, model_width : model_width + 2 * key_width]
    out_full = attn_full[:, model_width + 2 * key_width :]

    hidden_parts = ring.gather_all(hidden_own)
    hidden_all = jnp.concatenate(hidden_parts, 0)

    def ffn_slice(weight):
        return jnp.concatenate(
            [
                lax.dynamic_slice_in_dim(weight, place * ffn_half, ffn_half, 1),
                lax.dynamic_slice_in_dim(
                    weight, weight.shape[1] // 2 + place * ffn_half, ffn_half, 1
                ),
            ],
            1,
        )

    gate_own = ffn_slice(gate_weight)
    up_own = ffn_slice(up_weight)
    down_own = lax.dynamic_slice_in_dim(down_weight, place * ffn_half, ffn_half, 0)
    gate_mine = by_side(gate_own, swap_side(gate_own))
    up_mine = by_side(up_own, swap_side(up_own))
    down_mine = by_side(down_own, swap_side(down_own))

    devices = jnp.concatenate([ring.own_devices, ring.other_devices])
    pairs = jnp.sum(
        jnp.where(devices[:, None] == jnp.arange(n_ctx, dtype=jnp.int32)[None], pair_of[None], 0),
        1,
    )
    blocks_of = jnp.stack([pairs, 2 * n_ctx - 1 - pairs], 1).reshape(-1)
    listed = jnp.arange(2 * n_ctx, dtype=jnp.int32)
    place_of = jnp.sum(jnp.where(blocks_of[None, :] == listed[:, None], listed[None, :], 0), 1)
    offsets = jnp.arange(half_rows, dtype=jnp.int32)
    positions = (blocks_of[:, None] * half_rows + offsets[None, :]).reshape(-1)
    cosine, sine = rotary_tables(positions)
    cosine_own, sine_own = cosine[:local_rows], sine[:local_rows]
    starts = [blocks_of[0] * half_rows, blocks_of[1] * half_rows]

    normed_all, _ = normalize(hidden_all.astype(F32), gain_one)
    normed_all = normed_all.astype(BF16)
    inputs = hidden_own.astype(F32)
    normed_one, inverse_one = normalize(inputs, gain_one)
    normed_one = normed_one.astype(BF16)
    total_rows = hidden_all.shape[0]

    keyval = dot(normed_all, keyval_full) + jnp.concatenate([kbias, vbias])
    keys = rotary(keyval[:, :key_width].reshape(total_rows, KVH, HD), cosine, sine)
    keyval_rel = jnp.concatenate(
        [keys.reshape(total_rows, key_width).astype(BF16), keyval[:, key_width:].astype(BF16)], 1
    )
    keyval_order = jnp.take(
        keyval_rel.reshape(2 * n_ctx, half_rows, 2 * key_width), place_of, axis=0
    ).reshape(1, total_rows, 2 * key_width)
    queries = rotary(
        (dot(normed_one, query_full) + qbias).reshape(local_rows, H, HD), cosine_own, sine_own
    ).astype(BF16)

    tile_rows = math.gcd(1024, total_rows)
    query_groups = queries.reshape(1, local_rows, KVH, groups, HD)
    head_outs = []
    log_totals = []
    for slot in range(2):
        head_out, log_total = attend(
            query_groups[:, slot * half_rows : (slot + 1) * half_rows],
            starts[slot],
            keyval_order,
            tile_rows,
            key_width,
            score_scale,
        )
        head_outs.append(head_out)
        log_totals.append(log_total)
    heads = jnp.concatenate(
        [part.transpose(0, 3, 1, 2, 4).reshape(half_rows, H * HD) for part in head_outs], 0
    ).astype(BF16)
    resid = inputs + dot(heads, out_full)
    normed_two, inverse_two = normalize(resid, gain_two)
    normed_two = normed_two.astype(BF16)

    grad_all = jnp.concatenate(ring.gather_all(grad_own), 0)
    two_all = jnp.concatenate(ring.gather_all(normed_two), 0)
    gate_values = dot(two_all, gate_mine)
    up_values = dot(two_all, up_mine)
    sigmoid_gate = jax.nn.sigmoid(gate_values)
    silu_gate = gate_values * sigmoid_gate
    activation = (silu_gate * up_values).astype(BF16)
    grad_act = dot(grad_all, down_mine, 1, 1)
    grad_gate = (
        grad_act * up_values * sigmoid_gate * (1.0 + gate_values * (1.0 - sigmoid_gate))
    ).astype(BF16)
    grad_up = (grad_act * silu_gate).astype(BF16)
    grad_two_part = (dot(grad_gate, gate_mine, 1, 1) + dot(grad_up, up_mine, 1, 1)).astype(BF16)
    grad_two = ring.scatter_all(grad_two_part.reshape(n_ctx, local_rows, model_width))
    output_part = dot(activation, down_mine).astype(BF16)
    output = (
        resid + ring.scatter_all(output_part.reshape(n_ctx, local_rows, model_width))
    ).astype(BF16)

    down_part = dot(activation, grad_all, 0, 0).astype(BF16).reshape(2, ffn_half, model_width)

    def keep_send(first, second):
        return jnp.where(side == 0, first, second), jnp.where(side == 0, second, first)

    def fold(first, second):
        keep, send = keep_send(first, second)
        return (keep.astype(F32) + swap_side(send).astype(F32)).astype(BF16)

    def hidden_unit_grad(grad):
        full = dot(grad, two_all, 0, 0).astype(BF16)
        total = fold(full[:, :half_width], full[:, half_width:])
        return jnp.concatenate([total[:ffn_half], total[ffn_half:]], 1)

    down_total = fold(down_part[0], down_part[1])
    gate_total = hidden_unit_grad(grad_gate)
    up_total = hidden_unit_grad(grad_up)
    ffn_grads = lax.all_gather(
        jnp.stack([down_total, gate_total, up_total]), "ctx", axis=1, tiled=True
    )
    down_grad = ffn_grads[0].astype(F32)

    def unit_rows(gathered):
        return jnp.concatenate(
            [gathered[:, :half_width].T, gathered[:, half_width:].T], 1
        ).astype(F32)

    gate_grad = unit_rows(ffn_grads[1])
    up_grad = unit_rows(ffn_grads[2])

    gain_two_part = jnp.sum(grad_two * resid * inverse_two, 0)
    grad_resid = grad_own.astype(F32) + norm_back(resid, inverse_two, gain_two, grad_two)
    grad_attn = grad_resid.astype(BF16)
    out_part = dot(heads, grad_attn, 0, 0)
    grad_heads = dot(grad_attn, out_full, 1, 1).astype(BF16)
    grad_groups = grad_heads.reshape(1, local_rows, KVH, groups, HD)
    grad_keyval = jnp.zeros((1, total_rows, 2 * key_width), F32)
    grad_query_parts = []
    for slot in range(2):
        grad_slot = grad_groups[:, slot * half_rows : (slot + 1) * half_rows]
        delta = jnp.einsum("sqkgd,skgqd->skgq", grad_slot.astype(F32), head_outs[slot])
        grad_query, grad_keyval = attend_back(
            query_groups[:, slot * half_rows : (slot + 1) * half_rows],
            starts[slot],
            keyval_order,
            grad_slot,
            delta,
            log_totals[slot],
            grad_keyval,
            tile_rows,
            key_width,
            score_scale,
        )
        grad_query_parts.append(grad_query)
    grad_query_rot = jnp.concatenate(grad_query_parts, 1).reshape(local_rows, H, HD)
    grad_query_pre = rotary_back(grad_query_rot, cosine_own, sine_own).reshape(
        local_rows, H * HD
    )
    grad_keyval_rel = jnp.take(
        grad_keyval.reshape(2 * n_ctx, half_rows, 2 * key_width), blocks_of, axis=0
    ).reshape(total_rows, 2 * key_width)
    grad_key_pre = rotary_back(
        grad_keyval_rel[:, :key_width].reshape(total_rows, KVH, HD), cosine, sine
    ).reshape(total_rows, key_width)
    keyval_part32 = jnp.concatenate([grad_key_pre, grad_keyval_rel[:, key_width:]], 1)
    keyval_part = keyval_part32.astype(BF16)
    grad_keyval_own = ring.scatter_all(
        keyval_part.reshape(n_ctx, local_rows, 2 * key_width)
    ).astype(BF16)
    qbias_part = jnp.sum(grad_query_pre, 0)
    kvbias_part = jnp.sum(keyval_part32, 0)
    grad_query_pre = grad_query_pre.astype(BF16)
    query_part = dot(normed_one, grad_query_pre, 0, 0)
    keyval_grad_part = dot(normed_all, keyval_part, 0, 0)
    gain_one_part = (
        jnp.sum(query_part * query_full.astype(F32), 1)
        + jnp.sum(keyval_grad_part * keyval_full.astype(F32), 1)
    ) / gain_one

    grad_one = dot(grad_query_pre, query_full, 1, 1) + dot(grad_keyval_own, keyval_full, 1, 1)
    input_grad = (grad_resid + norm_back(inputs, inverse_one, gain_one, grad_one)).astype(BF16)

    pad_rows = 16
    wide = jnp.concatenate([query_part, keyval_grad_part, out_part], 1).astype(BF16)
    wide_cols = wide.shape[1]
    small_rows = []
    for index in range(2):
        pieces = [
            gain_one_part[index * half_width : (index + 1) * half_width],
            gain_two_part[index * half_width : (index + 1) * half_width],
            qbias_part[index * half_width : (index + 1) * half_width],
            kvbias_part[index * key_width // 2 : (index + 1) * key_width // 2],
            kvbias_part[key_width + index * key_width // 2 : key_width + (index + 1) * key_width // 2],
        ]
        row = jnp.concatenate(pieces)
        row = jnp.pad(row, (0, wide_cols - row.shape[0])).astype(BF16)
        small_rows.append(jnp.pad(row[None], ((0, pad_rows - 1), (0, 0))))
    packed = jnp.stack(
        [
            jnp.concatenate([wide[:half_width], small_rows[0]], 0),
            jnp.concatenate([wide[half_width:], small_rows[1]], 0),
        ]
    )
    half_cols = wide_cols // 2
    left, right = packed[:, :, :half_cols], packed[:, :, half_cols:]
    keep = jnp.where(core == 0, left, right)
    send = jnp.where(core == 0, right, left)
    chip_part = ring.add(keep, ring.swap_core(send))
    side_part = fold(chip_part[0], chip_part[1])
    pack_rows = side_part.shape[0]
    cut = half_cols // chips
    cuts = side_part.reshape(pack_rows, chips, cut).transpose(1, 0, 2)
    listed_cuts = jnp.take(cuts, ring.places, axis=0)
    total = ring.scatter([listed_cuts[i] for i in range(chips)]).astype(BF16)
    back = jnp.zeros((chips, pack_rows, cut), BF16)
    for index, part in enumerate(ring.gather(total)):
        back = lax.dynamic_update_index_in_dim(back, part, ring.places[index], 0)
    mine = back.transpose(1, 0, 2).reshape(pack_rows, half_cols)
    theirs = ring.swap_core(mine)
    whole = jnp.where(
        core == 0, jnp.concatenate([mine, theirs], 1), jnp.concatenate([theirs, mine], 1)
    ).astype(F32)
    wide_total = whole[:half_width]
    row = whole[half_width]
    bounds = []
    start = 0
    for size in small_sizes:
        bounds.append(row[start : start + size])
        start += size
    gain_one_total, gain_two_total, qbias_total, kbias_total, vbias_total = bounds
    cols = (
        model_width,
        model_width + key_width,
        model_width + 2 * key_width,
    )
    return (
        output[None],
        input_grad[None],
        gain_one_total,
        wide_total[:, : cols[0]],
        qbias_total,
        wide_total[:, cols[0] : cols[1]],
        kbias_total,
        wide_total[:, cols[1] : cols[2]],
        vbias_total,
        wide_total[:, cols[2] :],
        gain_two_total,
        gate_grad,
        up_grad,
        down_grad,
    )


def solution(mesh):
    in_specs = (
        P("fsdp", "ctx", None),
        P(),
        P("fsdp"),
        P("fsdp", None),
        P("fsdp"),
        P("fsdp", None),
        P("fsdp"),
        P("fsdp", None),
        P("fsdp"),
        P("fsdp", None),
        P("fsdp"),
        P("fsdp", None),
        P("fsdp", None),
        P("fsdp", None),
        P("fsdp", "ctx", None),
    )
    out_specs = (
        P("fsdp", "ctx", None),
        P("fsdp", "ctx", None),
        P("fsdp"),
        P("fsdp", None),
        P("fsdp"),
        P("fsdp", None),
        P("fsdp"),
        P("fsdp", None),
        P("fsdp"),
        P("fsdp", None),
        P("fsdp"),
        P("fsdp", None),
        P("fsdp", None),
        P("fsdp", None),
    )
    return jax.shard_map(
        on_device, mesh=mesh, in_specs=in_specs, out_specs=out_specs, check_vma=False
    )
```

time: 1600 us -> 665 us (0.42)
  blocking collectives: 655 us -> 0 us
  waiting for transfers between devices: 777 us -> 133 us
  local copies, waits for them, and re-layouts: 28.3 us -> 191 us
  other arithmetic: 21.8 us -> 128 us
  starting transfers between devices: 0.81 us -> 104 us
  matrix products: 92.5 us -> 62.2 us
    psum x1 -> x0, blocking collectives: 628 us -> none  [on_device(): lax.psum((gain_one_part, query_part, qbias_part, key_part, kbias_part, va...]
    reduce_scatter x8 -> x0, waiting for transfers between devices: 413 us -> none  [the longest x1 106 us: on_device(): lax.psum_scatter(up_grad.astype(jnp.bfloat16), 'fsdp', scatter_dimension=...]
    all_gather x6 -> x1, waiting for transfers between devices: 361 us -> 0.01 us  [on_device(): lax.all_gather(jnp.stack([down_total, gate_total, up_total]), 'ctx', axis...]
    ppermute x0 -> x103, waiting for transfers between devices: none -> 133 us  [the longest x32 54.3 us: send_up(): return lax.ppermute(block, 'ctx', self.up)]
    ppermute x0 -> x103, starting transfers between devices: none -> 104 us  [the longest x32 52.1 us: send_down(): return lax.ppermute(block, 'ctx', self.down)]
    unnamed x101 -> x206, local copies, waits for them, and re-layouts: 10.3 us -> 70.2 us
    dynamic_update_slice x0 -> x8, local copies, waits for them, and re-layouts: none -> 49.6 us  [on_device(): back = lax.dynamic_update_index_in_dim(back, part, ring.places[index], 0)]
    select_n x5 -> x13, other arithmetic: 2.32 us -> 42.3 us  [the longest x2 30.7 us: by_side(): jnp.where(side == 0, jnp.concatenate([own, other], axis), jnp.concatenate...]
  transfers between devices with their start and end apart: 14 -> 104, of which waited for: 12 -> 39; matrix products, arithmetic and copies ran while one was open for 6% -> 48% of each run, Pallas kernels for 0% -> 0%
where the time goes in v1:
time: 665 us; the launch traced here: 654 us
  local copies, waits for them, and re-layouts  191 us (29%)
  waiting for transfers between devices  133 us (20%)
  other arithmetic  128 us (19%)
  starting transfers between devices  104 us (16%)
  matrix products  62.2 us (9%)
  between operations  33.5 us (5%)
    unnamed x206, local copies, waits for them, and re-layouts  70.2 us
    ppermute x32, waiting for transfers between devices, send_up(): return lax.ppermute(block, 'ctx', self.up)  54.3 us
    ppermute x32, starting transfers between devices, send_down(): return lax.ppermute(block, 'ctx', self.down)  52.1 us
    dynamic_update_slice x8, local copies, waits for them, and re-layouts, on_device(): back = lax.dynamic_update_index_in_dim(back, part, ring.places[index], 0)  49.6 us
    dot_general x18, matrix products, dot(): lax.dot_general(left, right, (((left_dim,), (right_dim,)), ((), ())), pre...  42.5 us
    ppermute x9, waiting for transfers between devices, swap_side(): return lax.ppermute(value, 'fsdp', flip)  40.5 us
    ppermute x32, starting transfers between devices, send_up(): return lax.ppermute(block, 'ctx', self.up)  36.5 us
    ppermute x32, waiting for transfers between devices, send_down(): return lax.ppermute(block, 'ctx', self.down)  31.8 us
  transfers between devices with their start and end apart: 104, of which 39 were waited for; matrix products, arithmetic and copies ran while one was open for 48% of the time, Pallas kernels for 0%

profile of v1, /device:TPU:20, one launch (start us, length us, event | category | flops | bytes accessed | tf_op | source)
XLA Modules:
  0.0 653.7 jit_solution(980762955143256050)
XLA Ops:
  9.3 3.5 concatenate.276
  41.5 3.0 fusion.164
  117.6 3.3 fusion.116
  120.9 5.0 fusion.229
  128.2 3.8 maximum_select_fusion.1
  132.0 30.6 %maximum_select_fusion = bf16[896,2048]{0,1:T(8,128)(2,1)S(1)} fusion(bf16[448,2048]{0,1:T(8,128)(2,1)S(1)} %maximum_select_fusion.1, bf16[448,896]{0,1:T(8,128)(2,1)S(1)} %copy.160, bf16[448,128]{0,1:T(8,128)(2,1)S(1)} %copy-done.35, bf16[448,128]{0,1:T(8,128)(2,1)S(1)} %copy.158, bf16[448,896]{0,1:T(8,128)(2,1)S(1)} %copy.157, pred[]{:T(512)S(6)} %eq.30), kind=kLoop, calls=%fused_computation.137 | loop fusion | flops 38535168 | bytes 7340033 | tf_op jit(solution)/shard_map/jit(_where)/select_n | solution.py:272
  170.7 3.4 while.56
  175.6 6.0 while.57
  187.4 5.5 collective-permute-done.19
  195.0 4.6 collective-permute-done.21
  201.7 4.1 collective-permute-done.23
  208.2 2.5 collective-permute-done.25
  215.2 2.8 fusion.248
  218.0 3.8 multiply_convert_fusion.1
  224.8 3.5 fusion.247
  228.4 3.6 add_convert_fusion
  237.0 3.5 convolution_convert_fusion
  245.7 7.0 %collective-permute-done.102 = bf16[304,448]{1,0:T(8,128)(2,1)S(1)} collective-permute-done((bf16[304,448]{1,0:T(8,128)(2,1)S(1)}, bf16[304,448]{1,0:T(8,128)(2,1)S(1)}, u32[]{:S(2)}, u32[]{:S(2)}) %collective-permute-start.102) | collective-permute-done | bytes 272416 | tf_op jit(solution)/shard_map/ppermute | solution.py:269
  253.0 6.4 collective-permute-done.101
  259.9 4.7 collective-permute-done.100
  265.7 2.5 fusion.122
  276.7 2.5 collective-permute-done.39
  279.1 4.0 collective-permute-done.43
  285.4 4.6 collective-permute-done.65
  290.0 5.9 collective-permute-start.66
  295.9 6.5 collective-permute-done.40
  302.5 7.9 %collective-permute-start.41 = (bf16[128,896]{1,0:T(8,128)(2,1)S(1)}, bf16[128,896]{1,0:T(8,128)(2,1)S(1)}, u32[]{:S(2)}, u32[]{:S(2)}) collective-permute-start(bf16[128,896]{1,0:T(8,128)(2,1)S(1)} %fusion.185), channel_id=1, source_target_pairs={{0,8},{2,10},{8,16},{10,18},{16,24},{18,26},{24,28},{26,30},{28,20... | collective-permute-start | bytes 688136 | tf_op jit(solution)/shard_map/ppermute | solution.py:91
  312.0 7.1 %collective-permute-start.67 = (bf16[128,896]{1,0:T(8,128)(2,1)S(1)}, bf16[128,896]{1,0:T(8,128)(2,1)S(1)}, u32[]{:S(2)}, u32[]{:S(2)}) collective-permute-start(bf16[128,896]{1,0:T(8,128)(2,1)S(1)} %get-tuple-element.618), channel_id=1, source_target_pairs={{0,8},{2,10},{8,16},{10,18},{16,24},{18,26},{24,28},{26,30},{28,20... | collective-permute-start | bytes 688136 | tf_op jit(solution)/shard_map/ppermute | solution.py:91
  319.0 3.3 collective-permute-done.41
  322.6 2.4 collective-permute-start.42
  325.1 2.4 collective-permute-start.71
  327.5 3.9 collective-permute-done.45
  333.6 7.6 %collective-permute-done.71 = bf16[128,896]{1,0:T(8,128)(2,1)S(1)} collective-permute-done((bf16[128,896]{1,0:T(8,128)(2,1)S(1)}, bf16[128,896]{1,0:T(8,128)(2,1)S(1)}, u32[]{:S(2)}, u32[]{:S(2)}) %collective-permute-start.71) | collective-permute-done | bytes 229408 | tf_op jit(solution)/shard_map/ppermute | solution.py:94
  341.4 11.5 %collective-permute-done.46 = bf16[128,896]{1,0:T(8,128)(2,1)S(1)} collective-permute-done((bf16[128,896]{1,0:T(8,128)(2,1)S(1)}, bf16[128,896]{1,0:T(8,128)(2,1)S(1)}, u32[]{:S(2)}, u32[]{:S(2)}) %collective-permute-start.46) | collective-permute-done | bytes 229408 | tf_op jit(solution)/shard_map/ppermute | solution.py:94
  359.4 6.4 while.58
  370.2 10.1 %while.59 = (s32[]{:T(128)}, f32[1,64,2,7,64]{1,4,3,2,0:T(8,128)}, f32[1,2048,256]{1,2,0:T(8,128)S(1)}, s32[]{:T(128)}, bf16[1,2048,256]{1,2,0:T(8,128)(2,1)S(1)...) while((s32[]{:T(128)}, f32[1,64,2,7,64]{1,4,3,2,0:T(8,128)}, ...), condition=%wide.region_17.18_spmd.clone, body=%wide.region_16.17_spmd.clone.sunk | while | flops 597214272 | bytes 25972024 | solution.py:240
  382.1 2.4 gather_fusion.1
  402.9 6.9 %pad_maximum_fusion = bf16[896,2048]{0,1:T(8,128)(2,1)S(1)} fusion(bf16[896,896]{0,1:T(8,128)(2,1)S(1)} %convolution_convert_fusion.1, bf16[896,256]{0,1:T(8,128)(2,1)S(1)} %copy-done.45, bf16[896,896]{0,1:T(8,128)(2,1)S(1)} %copy-done.34), kind=kLoop, calls=%fused_computation.138 | loop fusion | flops 11010048 | bytes 7340032 | tf_op jit(solution)/shard_map/concatenate | solution.py:492
  414.7 4.1 copy.185
  418.9 4.2 collective-permute-done.81
  423.2 3.9 copy.186
  427.0 2.6 add_convert_fusion.1
  435.4 22.4 %collective-permute-done.82 = bf16[464,1024]{1,0:T(8,128)(2,1)} collective-permute-done((bf16[464,1024]{1,0:T(8,128)(2,1)}, bf16[464,1024]{1,0:T(8,128)(2,1)}, u32[]{:S(2)}, u32[]{:S(2)}) %collective-permute-start.82) | collective-permute-done | bytes 950304 | tf_op jit(solution)/shard_map/ppermute | solution.py:269
  460.1 2.6 fusion.130
  462.7 2.9 gather_fusion.2
  480.0 2.5 collective-permute-done.84
  485.6 3.1 collective-permute-done.85
  488.8 2.7 collective-permute-start.89
  494.3 2.5 collective-permute-start.90
  509.5 2.9 collective-permute-done.93
  540.0 6.4 dynamic_update_slice.31
  546.8 6.2 dynamic_update_slice.32
  553.0 6.2 dynamic_update_slice.33
  560.4 6.2 dynamic_update_slice.34
  566.6 6.2 dynamic_update_slice.35
  573.1 6.2 dynamic_update_slice.36
  579.3 6.2 dynamic_update_slice.37
  585.8 6.2 dynamic_update_slice.38
  601.1 8.7 %fusion.119 = (f32[2432,896]{1,0:T(8,128)}, bf16[2432,896]{1,0:T(8,128)(2,1)}, bf16[2432,896]{1,0:T(8,128)(2,1)S(1)}) fusion(bf16[3,2432,896]{2,1,0:T(8,128)(2,1)} %all-gather.2.cloned.1.call-done), kind=kLoop, calls=%fused_computation.128 | loop fusion | flops 2179072 | bytes 30507008 | tf_op jit(solution)/shard_map/convert_element_type | solution.py:429
  611.3 5.2 maximum_convert_fusion
  616.5 10.5 %copy.197 = f32[448,4864]{1,0:T(8,128)} copy(f32[448,4864]{0,1:T(8,128)} %maximum_convert_fusion) | data formatting | bytes 17432576
  627.0 3.9 slice_bitcast_fusion.4
  630.9 5.2 maximum_convert_fusion.1
  636.1 10.3 %copy.198 = f32[448,4864]{1,0:T(8,128)} copy(f32[448,4864]{0,1:T(8,128)} %maximum_convert_fusion.1) | data formatting | bytes 17432576
  (679 shorter events, 286.6 us)
Async XLA Ops:
  7.2 594.0 %all-gather.2.cloned.1.call-start = ((), (), s32[]{:S(2)}) async-start(), calls=%async_computation | async-start | bytes 13891584 | tf_op jit(solution)/shard_map/all_gather | solution.py:426
  7.2 45.6 %collective-permute-start = (bf16[128,896]{1,0:T(8,128)(2,1)}, bf16[128,896]{1,0:T(8,128)(2,1)}, u32[]{:S(2)}, u32[]{:S(2)}) collective-permute-start(bf16[128,896]{1,0:T(8,128)(2,1)} %bitcast.833), channel_id=1, source_target_pairs={{0,8},{2,10},{8,16},{10,18},{16,24},{18,26},{24,28},{26,30},{28,20... | collective-permute-start | bytes 688136 | tf_op jit(solution)/shard_map/ppermute | solution.py:91
  7.7 46.9 %collective-permute-start.1 = (bf16[128,896]{1,0:T(8,128)(2,1)}, bf16[128,896]{1,0:T(8,128)(2,1)}, u32[]{:S(2)}, u32[]{:S(2)}) collective-permute-start(bf16[128,896]{1,0:T(8,128)(2,1)} %bitcast.834), channel_id=1, source_target_pairs={{8,0},{10,2},{16,8},{18,10},{24,16},{26,18},{28,24},{30,26},{20,28... | collective-permute-start | bytes 688136 | tf_op jit(solution)/shard_map/ppermute | solution.py:94
  9.3 79.8 %collective-permute-start.8 = (bf16[128,896]{1,0:T(8,128)(2,1)}, bf16[128,896]{1,0:T(8,128)(2,1)}, u32[]{:S(2)}, u32[]{:S(2)}) collective-permute-start(bf16[128,896]{1,0:T(8,128)(2,1)} %bitcast.835), channel_id=1, source_target_pairs={{0,2},{2,0},{4,6},{6,4},{8,10},{10,8},{12,14},{14,12},{16,18},{18,... | collective-permute-start | bytes 688136 | tf_op jit(solution)/shard_map/ppermute | solution.py:97
  12.8 36.7 %collective-permute-start.16 = (bf16[1472]{0:T(1024)(128)(2,1)S(1)}, bf16[1472]{0:T(1024)(128)(2,1)S(1)}, u32[]{:S(2)}, u32[]{:S(2)}) collective-permute-start(bf16[1472]{0:T(1024)(128)(2,1)S(1)} %concatenate.276), channel_id=1, source_target_pairs={{0,1},{1,0},{2,3},{3,2},{4,5},{5,4},{6,7},{7,6},{8,9},{9,8},{10,11... | collective-permute-start | bytes 8840 | tf_op jit(solution)/shard_map/ppermute | solution.py:269
  14.3 42.4 %collective-permute-start.47 = (bf16[128,896]{1,0:T(8,128)(2,1)}, bf16[128,896]{1,0:T(8,128)(2,1)}, u32[]{:S(2)}, u32[]{:S(2)}) collective-permute-start(bf16[128,896]{1,0:T(8,128)(2,1)} %bitcast.845), channel_id=1, source_target_pairs={{0,8},{2,10},{8,16},{10,18},{16,24},{18,26},{24,28},{26,30},{28,20... | collective-permute-start | bytes 688136 | tf_op jit(solution)/shard_map/ppermute | solution.py:91
  49.5 10.4 %collective-permute-start.48 = (bf16[128,896]{1,0:T(8,128)(2,1)}, bf16[128,896]{1,0:T(8,128)(2,1)S(1)}, u32[]{:S(2)}, u32[]{:S(2)}) collective-permute-start(bf16[128,896]{1,0:T(8,128)(2,1)} %bitcast.846), channel_id=1, source_target_pairs={{8,0},{10,2},{16,8},{18,10},{24,16},{26,18},{28,24},{30,26},{20,28... | collective-permute-start | bytes 688136 | tf_op jit(solution)/shard_map/ppermute | solution.py:94
  52.9 48.9 %collective-permute-start.55 = (bf16[128,896]{1,0:T(8,128)(2,1)}, bf16[128,896]{1,0:T(8,128)(2,1)S(1)}, u32[]{:S(2)}, u32[]{:S(2)}) collective-permute-start(bf16[128,896]{1,0:T(8,128)(2,1)} %bitcast.847), channel_id=1, source_target_pairs={{0,2},{2,0},{4,6},{6,4},{8,10},{10,8},{12,14},{14,12},{16,18},{18,... | collective-permute-start | bytes 688136 | tf_op jit(solution)/shard_map/ppermute | solution.py:97
  54.6 8.4 %collective-permute-start.2 = (bf16[128,896]{1,0:T(8,128)(2,1)}, bf16[128,896]{1,0:T(8,128)(2,1)S(1)}, u32[]{:S(2)}, u32[]{:S(2)}) collective-permute-start(bf16[128,896]{1,0:T(8,128)(2,1)} %collective-permute-done), channel_id=1, source_target_pairs={{0,8},{2,10},{8,16},{10,18},{16,24},{18,26},{24,28},{26,30},{28,20... | collective-permute-start | bytes 688136 | tf_op jit(solution)/shard_map/ppermute | solution.py:91
  56.7 8.5 %collective-permute-start.3 = (bf16[128,896]{1,0:T(8,128)(2,1)}, bf16[128,896]{1,0:T(8,128)(2,1)S(1)}, u32[]{:S(2)}, u32[]{:S(2)}) collective-permute-start(bf16[128,896]{1,0:T(8,128)(2,1)} %collective-permute-done.1), channel_id=1, source_target_pairs={{8,0},{10,2},{16,8},{18,10},{24,16},{26,18},{28,24},{30,26},{20,28... | collective-permute-start | bytes 688136 | tf_op jit(solution)/shard_map/ppermute | solution.py:94
  59.9 8.5 %collective-permute-start.49 = (bf16[128,896]{1,0:T(8,128)(2,1)}, bf16[128,896]{1,0:T(8,128)(2,1)S(1)}, u32[]{:S(2)}, u32[]{:S(2)}) collective-permute-start(bf16[128,896]{1,0:T(8,128)(2,1)} %collective-permute-done.47), channel_id=1, source_target_pairs={{0,8},{2,10},{8,16},{10,18},{16,24},{18,26},{24,28},{26,30},{28,20... | collective-permute-start | bytes 688136 | tf_op jit(solution)/shard_map/ppermute | solution.py:91
  63.0 7.9 %collective-permute-start.50 = (bf16[128,896]{1,0:T(8,128)(2,1)S(1)}, bf16[128,896]{1,0:T(8,128)(2,1)S(1)}, u32[]{:S(2)}, u32[]{:S(2)}) collective-permute-start(bf16[128,896]{1,0:T(8,128)(2,1)S(1)} %collective-permute-done.48), channel_id=1, source_target_pairs={{8,0},{10,2},{16,8},{18,10},{24,16},{26,18},{28,24},{30,26},{20,28... | collective-permute-start | bytes 688136 | tf_op jit(solution)/shard_map/ppermute | solution.py:94
  65.2 8.6 %collective-permute-start.4 = (bf16[128,896]{1,0:T(8,128)(2,1)S(1)}, bf16[128,896]{1,0:T(8,128)(2,1)}, u32[]{:S(2)}, u32[]{:S(2)}) collective-permute-start(bf16[128,896]{1,0:T(8,128)(2,1)S(1)} %collective-permute-done.2), channel_id=1, source_target_pairs={{0,8},{2,10},{8,16},{10,18},{16,24},{18,26},{24,28},{26,30},{28,20... | collective-permute-start | bytes 688136 | tf_op jit(solution)/shard_map/ppermute | solution.py:91
  68.4 6.9 %collective-permute-start.5 = (bf16[128,896]{1,0:T(8,128)(2,1)S(1)}, bf16[128,896]{1,0:T(8,128)(2,1)}, u32[]{:S(2)}, u32[]{:S(2)}) collective-permute-start(bf16[128,896]{1,0:T(8,128)(2,1)S(1)} %collective-permute-done.3), channel_id=1, source_target_pairs={{8,0},{10,2},{16,8},{18,10},{24,16},{26,18},{28,24},{30,26},{20,28... | collective-permute-start | bytes 688136 | tf_op jit(solution)/shard_map/ppermute | solution.py:94
  70.9 8.4 %collective-permute-start.51 = (bf16[128,896]{1,0:T(8,128)(2,1)S(1)}, bf16[128,896]{1,0:T(8,128)(2,1)S(1)}, u32[]{:S(2)}, u32[]{:S(2)}) collective-permute-start(bf16[128,896]{1,0:T(8,128)(2,1)S(1)} %collective-permute-done.49), channel_id=1, source_target_pairs={{0,8},{2,10},{8,16},{10,18},{16,24},{18,26},{24,28},{26,30},{28,20... | collective-permute-start | bytes 688136 | tf_op jit(solution)/shard_map/ppermute | solution.py:91
  73.8 33.0 %collective-permute-start.17 = (bf16[224,2048]{1,0:T(8,128)(2,1)S(1)}, bf16[224,2048]{1,0:T(8,128)(2,1)S(1)}, u32[]{:S(2)}, u32[]{:S(2)}) collective-permute-start(bf16[224,2048]{1,0:T(8,128)(2,1)S(1)} %copy-done.36), channel_id=1, source_target_pairs={{0,1},{1,0},{2,3},{3,2},{4,5},{5,4},{6,7},{7,6},{8,9},{9,8},{10,11... | collective-permute-start | bytes 2752520 | tf_op jit(solution)/shard_map/ppermute | solution.py:269
  75.3 7.0 %collective-permute-start.52 = (bf16[128,896]{1,0:T(8,128)(2,1)S(1)}, bf16[128,896]{1,0:T(8,128)(2,1)S(1)}, u32[]{:S(2)}, u32[]{:S(2)}) collective-permute-start(bf16[128,896]{1,0:T(8,128)(2,1)S(1)} %collective-permute-done.50), channel_id=1, source_target_pairs={{8,0},{10,2},{16,8},{18,10},{24,16},{26,18},{28,24},{30,26},{20,28... | collective-permute-start | bytes 688136 | tf_op jit(solution)/shard_map/ppermute | solution.py:94
  84.4 36.5 %collective-permute-start.37 = (bf16[152,896]{1,0:T(8,128)(2,1)}, bf16[152,896]{1,0:T(8,128)(2,1)}, u32[]{:S(2)}, u32[]{:S(2)}) collective-permute-start(bf16[152,896]{1,0:T(8,128)(2,1)} %constant_dynamic-slice_fusion.8), channel_id=1, source_target_pairs={{0,1},{1,0},{2,3},{3,2},{4,5},{5,4},{6,7},{7,6},{8,9},{9,8},{10,11... | collective-permute-start | bytes 817160 | tf_op jit(solution)/shard_map/ppermute | solution.py:269
  98.3 116.9 %collective-permute-start.36 = (bf16[448,304]{1,0:T(8,128)(2,1)}, bf16[448,304]{1,0:T(8,128)(2,1)}, u32[]{:S(2)}, u32[]{:S(2)}) collective-permute-start(bf16[448,304]{1,0:T(8,128)(2,1)} %pad_maximum_fusion.10), channel_id=1, source_target_pairs={{0,1},{1,0},{2,3},{3,2},{4,5},{5,4},{6,7},{7,6},{8,9},{9,8},{10,11... | collective-permute-start | bytes 817160 | tf_op jit(solution)/shard_map/ppermute | solution.py:269
  104.9 6.2 collective-permute-start.13
  105.7 7.1 %collective-permute-start.14 = (bf16[128,896]{1,0:T(8,128)(2,1)}, bf16[128,896]{1,0:T(8,128)(2,1)}, u32[]{:S(2)}, u32[]{:S(2)}) collective-permute-start(bf16[128,896]{1,0:T(8,128)(2,1)} %collective-permute-done.5), channel_id=1, source_target_pairs={{0,2},{2,0},{4,6},{6,4},{8,10},{10,8},{12,14},{14,12},{16,18},{18,... | collective-permute-start | bytes 688136 | tf_op jit(solution)/shard_map/ppermute | solution.py:97
  107.8 110.2 %collective-permute-start.35 = (bf16[448,304]{1,0:T(8,128)(2,1)}, bf16[448,304]{1,0:T(8,128)(2,1)}, u32[]{:S(2)}, u32[]{:S(2)}) collective-permute-start(bf16[448,304]{1,0:T(8,128)(2,1)} %pad_maximum_fusion.9), channel_id=1, source_target_pairs={{0,1},{1,0},{2,3},{3,2},{4,5},{5,4},{6,7},{7,6},{8,9},{9,8},{10,11... | collective-permute-start | bytes 817160 | tf_op jit(solution)/shard_map/ppermute | solution.py:269
  116.9 9.1 %collective-permute-start.18 = (bf16[224,2048]{1,0:T(8,128)(2,1)}, bf16[224,2048]{1,0:T(8,128)(2,1)}, u32[]{:S(2)}, u32[]{:S(2)}) collective-permute-start(bf16[224,2048]{1,0:T(8,128)(2,1)} %copy-done.37), channel_id=1, source_target_pairs={{0,2},{2,0},{4,6},{6,4},{8,10},{10,8},{12,14},{14,12},{16,18},{18,... | collective-permute-start | bytes 2752520 | tf_op jit(solution)/shard_map/ppermute | solution.py:97
  185.3 7.6 %collective-permute-start.19 = (bf16[128,896]{1,0:T(8,128)(2,1)S(1)}, bf16[128,896]{1,0:T(8,128)(2,1)S(1)}, u32[]{:S(2)}, u32[]{:S(2)}) collective-permute-start(bf16[128,896]{1,0:T(8,128)(2,1)S(1)} %get-tuple-element.571), channel_id=1, source_target_pairs={{0,8},{2,10},{8,16},{10,18},{16,24},{18,26},{24,28},{26,30},{28,20... | collective-permute-start | bytes 688136 | tf_op jit(solution)/shard_map/ppermute | solution.py:91
  185.8 7.6 %collective-permute-start.20 = (bf16[128,896]{1,0:T(8,128)(2,1)S(1)}, bf16[128,896]{1,0:T(8,128)(2,1)S(1)}, u32[]{:S(2)}, u32[]{:S(2)}) collective-permute-start(bf16[128,896]{1,0:T(8,128)(2,1)S(1)} %get-tuple-element.571), channel_id=1, source_target_pairs={{8,0},{10,2},{16,8},{18,10},{24,16},{26,18},{28,24},{30,26},{20,28... | collective-permute-start | bytes 688136 | tf_op jit(solution)/shard_map/ppermute | solution.py:94
  187.4 24.1 %collective-permute-start.27 = (bf16[128,896]{1,0:T(8,128)(2,1)S(1)}, bf16[128,896]{1,0:T(8,128)(2,1)S(1)}, u32[]{:S(2)}, u32[]{:S(2)}) collective-permute-start(bf16[128,896]{1,0:T(8,128)(2,1)S(1)} %get-tuple-element.571), channel_id=1, source_target_pairs={{0,2},{2,0},{4,6},{6,4},{8,10},{10,8},{12,14},{14,12},{16,18},{18,... | collective-permute-start | bytes 688136 | tf_op jit(solution)/shard_map/ppermute | solution.py:97
  192.9 6.7 %collective-permute-start.21 = (bf16[128,896]{1,0:T(8,128)(2,1)S(1)}, bf16[128,896]{1,0:T(8,128)(2,1)S(1)}, u32[]{:S(2)}, u32[]{:S(2)}) collective-permute-start(bf16[128,896]{1,0:T(8,128)(2,1)S(1)} %collective-permute-done.19), channel_id=1, source_target_pairs={{0,8},{2,10},{8,16},{10,18},{16,24},{18,26},{24,28},{26,30},{28,20... | collective-permute-start | bytes 688136 | tf_op jit(solution)/shard_map/ppermute | solution.py:91
  193.4 6.7 %collective-permute-start.22 = (bf16[128,896]{1,0:T(8,128)(2,1)S(1)}, bf16[128,896]{1,0:T(8,128)(2,1)S(1)}, u32[]{:S(2)}, u32[]{:S(2)}) collective-permute-start(bf16[128,896]{1,0:T(8,128)(2,1)S(1)} %collective-permute-done.20), channel_id=1, source_target_pairs={{8,0},{10,2},{16,8},{18,10},{24,16},{26,18},{28,24},{30,26},{20,28... | collective-permute-start | bytes 688136 | tf_op jit(solution)/shard_map/ppermute | solution.py:94
  200.1 6.2 collective-permute-start.24
  234.2 31.5 %collective-permute-start.63 = (bf16[8,128,896]{2,1,0:T(8,128)(2,1)}, bf16[8,128,896]{2,1,0:T(8,128)(2,1)}, u32[]{:S(2)}, u32[]{:S(2)}) collective-permute-start(bf16[8,128,896]{2,1,0:T(8,128)(2,1)} %bitcast.40), channel_id=1, source_target_pairs={{0,2},{2,0},{4,6},{6,4},{8,10},{10,8},{12,14},{14,12},{16,18},{18,... | collective-permute-start | bytes 5505032 | tf_op jit(solution)/shard_map/ppermute | solution.py:97
  242.0 28.3 %collective-permute-start.38 = (bf16[8,128,896]{2,1,0:T(8,128)(2,1)}, bf16[8,128,896]{2,1,0:T(8,128)(2,1)}, u32[]{:S(2)}, u32[]{:S(2)}) collective-permute-start(bf16[8,128,896]{2,1,0:T(8,128)(2,1)} %bitcast.25), channel_id=1, source_target_pairs={{0,2},{2,0},{4,6},{6,4},{8,10},{10,8},{12,14},{14,12},{16,18},{18,... | collective-permute-start | bytes 5505032 | tf_op jit(solution)/shard_map/ppermute | solution.py:97
  242.4 10.3 %collective-permute-start.102 = (bf16[304,448]{1,0:T(8,128)(2,1)S(1)}, bf16[304,448]{1,0:T(8,128)(2,1)S(1)}, u32[]{:S(2)}, u32[]{:S(2)}) collective-permute-start(bf16[304,448]{1,0:T(8,128)(2,1)S(1)} %broadcast_select_fusion.3), channel_id=1, source_target_pairs={{0,1},{1,0},{2,3},{3,2},{4,5},{5,4},{6,7},{7,6},{8,9},{9,8},{10,11... | collective-permute-start | bytes 817160 | tf_op jit(solution)/shard_map/ppermute | solution.py:269
  243.5 15.8 %collective-permute-start.101 = (bf16[304,448]{1,0:T(8,128)(2,1)S(1)}, bf16[304,448]{1,0:T(8,128)(2,1)S(1)}, u32[]{:S(2)}, u32[]{:S(2)}) collective-permute-start(bf16[304,448]{1,0:T(8,128)(2,1)S(1)} %broadcast_select_fusion.4), channel_id=1, source_target_pairs={{0,1},{1,0},{2,3},{3,2},{4,5},{5,4},{6,7},{7,6},{8,9},{9,8},{10,11... | collective-permute-start | bytes 817160 | tf_op jit(solution)/shard_map/ppermute | solution.py:269
  244.7 19.8 %collective-permute-start.100 = (bf16[152,896]{1,0:T(8,128)(2,1)S(1)}, bf16[152,896]{1,0:T(8,128)(2,1)S(1)}, u32[]{:S(2)}, u32[]{:S(2)}) collective-permute-start(bf16[152,896]{1,0:T(8,128)(2,1)S(1)} %broadcast_select_fusion.5), channel_id=1, source_target_pairs={{0,1},{1,0},{2,3},{3,2},{4,5},{5,4},{6,7},{7,6},{8,9},{9,8},{10,11... | collective-permute-start | bytes 817160 | tf_op jit(solution)/shard_map/ppermute | solution.py:269
  272.3 6.8 %collective-permute-start.39 = (bf16[64,896]{1,0:T(8,128)(2,1)S(1)}, bf16[64,896]{1,0:T(8,128)(2,1)S(1)}, u32[]{:S(2)}, u32[]{:S(2)}) collective-permute-start(bf16[64,896]{1,0:T(8,128)(2,1)S(1)} %get-tuple-element.630), channel_id=1, source_target_pairs={{0,8},{2,10},{8,16},{10,18},{16,24},{18,26},{24,28},{26,30},{28,20... | collective-permute-start | bytes 344072 | tf_op jit(solution)/shard_map/ppermute | solution.py:91
  272.8 10.3 %collective-permute-start.43 = (bf16[64,896]{1,0:T(8,128)(2,1)S(1)}, bf16[64,896]{1,0:T(8,128)(2,1)S(1)}, u32[]{:S(2)}, u32[]{:S(2)}) collective-permute-start(bf16[64,896]{1,0:T(8,128)(2,1)S(1)} %get-tuple-element.631), channel_id=1, source_target_pairs={{8,0},{10,2},{16,8},{18,10},{24,16},{26,18},{28,24},{30,26},{20,28... | collective-permute-start | bytes 344072 | tf_op jit(solution)/shard_map/ppermute | solution.py:94
  274.5 15.4 %collective-permute-start.65 = (bf16[128,896]{1,0:T(8,128)(2,1)S(1)}, bf16[128,896]{1,0:T(8,128)(2,1)S(1)}, u32[]{:S(2)}, u32[]{:S(2)}) collective-permute-start(bf16[128,896]{1,0:T(8,128)(2,1)S(1)} %pad_maximum_fusion.16), channel_id=1, source_target_pairs={{0,8},{2,10},{8,16},{10,18},{16,24},{18,26},{24,28},{26,30},{28,20... | collective-permute-start | bytes 688136 | tf_op jit(solution)/shard_map/ppermute | solution.py:91
  275.3 35.1 %collective-permute-start.69 = (bf16[128,896]{1,0:T(8,128)(2,1)S(1)}, bf16[128,896]{1,0:T(8,128)(2,1)S(1)}, u32[]{:S(2)}, u32[]{:S(2)}) collective-permute-start(bf16[128,896]{1,0:T(8,128)(2,1)S(1)} %pad_maximum_fusion.17), channel_id=1, source_target_pairs={{8,0},{10,2},{16,8},{18,10},{24,16},{26,18},{28,24},{30,26},{20,28... | collective-permute-start | bytes 688136 | tf_op jit(solution)/shard_map/ppermute | solution.py:94
  283.2 19.2 %collective-permute-start.40 = (bf16[128,896]{1,0:T(8,128)(2,1)S(1)}, bf16[128,896]{1,0:T(8,128)(2,1)S(1)}, u32[]{:S(2)}, u32[]{:S(2)}) collective-permute-start(bf16[128,896]{1,0:T(8,128)(2,1)S(1)} %pad_maximum_fusion.13), channel_id=1, source_target_pairs={{0,8},{2,10},{8,16},{10,18},{16,24},{18,26},{24,28},{26,30},{28,20... | collective-permute-start | bytes 688136 | tf_op jit(solution)/shard_map/ppermute | solution.py:91
  283.3 35.7 %collective-permute-start.44 = (bf16[128,896]{1,0:T(8,128)(2,1)S(1)}, bf16[128,896]{1,0:T(8,128)(2,1)S(1)}, u32[]{:S(2)}, u32[]{:S(2)}) collective-permute-start(bf16[128,896]{1,0:T(8,128)(2,1)S(1)} %pad_maximum_fusion.14), channel_id=1, source_target_pairs={{8,0},{10,2},{16,8},{18,10},{24,16},{26,18},{28,24},{30,26},{20,28... | collective-permute-start | bytes 688136 | tf_op jit(solution)/shard_map/ppermute | solution.py:94
  290.0 21.8 %collective-permute-start.66 = (bf16[128,896]{1,0:T(8,128)(2,1)S(1)}, bf16[128,896]{1,0:T(8,128)(2,1)S(1)}, u32[]{:S(2)}, u32[]{:S(2)}) collective-permute-start(bf16[128,896]{1,0:T(8,128)(2,1)S(1)} %fusion.180), channel_id=1, source_target_pairs={{0,8},{2,10},{8,16},{10,18},{16,24},{18,26},{24,28},{26,30},{28,20... | collective-permute-start | bytes 688136 | tf_op jit(solution)/shard_map/ppermute | solution.py:91
  302.5 19.8 %collective-permute-start.41 = (bf16[128,896]{1,0:T(8,128)(2,1)S(1)}, bf16[128,896]{1,0:T(8,128)(2,1)S(1)}, u32[]{:S(2)}, u32[]{:S(2)}) collective-permute-start(bf16[128,896]{1,0:T(8,128)(2,1)S(1)} %fusion.185), channel_id=1, source_target_pairs={{0,8},{2,10},{8,16},{10,18},{16,24},{18,26},{24,28},{26,30},{28,20... | collective-permute-start | bytes 688136 | tf_op jit(solution)/shard_map/ppermute | solution.py:91
  311.9 13.1 %collective-permute-start.70 = (bf16[128,896]{1,0:T(8,128)(2,1)S(1)}, bf16[128,896]{1,0:T(8,128)(2,1)S(1)}, u32[]{:S(2)}, u32[]{:S(2)}) collective-permute-start(bf16[128,896]{1,0:T(8,128)(2,1)S(1)} %get-tuple-element.619), channel_id=1, source_target_pairs={{8,0},{10,2},{16,8},{18,10},{24,16},{26,18},{28,24},{30,26},{20,28... | collective-permute-start | bytes 688136 | tf_op jit(solution)/shard_map/ppermute | solution.py:94
  312.0 21.6 %collective-permute-start.67 = (bf16[128,896]{1,0:T(8,128)(2,1)S(1)}, bf16[128,896]{1,0:T(8,128)(2,1)S(1)}, u32[]{:S(2)}, u32[]{:S(2)}) collective-permute-start(bf16[128,896]{1,0:T(8,128)(2,1)S(1)} %get-tuple-element.618), channel_id=1, source_target_pairs={{0,8},{2,10},{8,16},{10,18},{16,24},{18,26},{24,28},{26,30},{28,20... | collective-permute-start | bytes 688136 | tf_op jit(solution)/shard_map/ppermute | solution.py:91
  322.4 9.0 %collective-permute-start.45 = (bf16[128,896]{1,0:T(8,128)(2,1)S(1)}, bf16[128,896]{1,0:T(8,128)(2,1)S(1)}, u32[]{:S(2)}, u32[]{:S(2)}) collective-permute-start(bf16[128,896]{1,0:T(8,128)(2,1)S(1)} %get-tuple-element.627), channel_id=1, source_target_pairs={{8,0},{10,2},{16,8},{18,10},{24,16},{26,18},{28,24},{30,26},{20,28... | collective-permute-start | bytes 688136 | tf_op jit(solution)/shard_map/ppermute | solution.py:94
  322.6 18.8 %collective-permute-start.42 = (bf16[128,896]{1,0:T(8,128)(2,1)S(1)}, bf16[128,896]{1,0:T(8,128)(2,1)S(1)}, u32[]{:S(2)}, u32[]{:S(2)}) collective-permute-start(bf16[128,896]{1,0:T(8,128)(2,1)S(1)} %get-tuple-element.626), channel_id=1, source_target_pairs={{0,8},{2,10},{8,16},{10,18},{16,24},{18,26},{24,28},{26,30},{28,20... | collective-permute-start | bytes 688136 | tf_op jit(solution)/shard_map/ppermute | solution.py:91
  325.1 16.1 %collective-permute-start.71 = (bf16[128,896]{1,0:T(8,128)(2,1)S(1)}, bf16[128,896]{1,0:T(8,128)(2,1)S(1)}, u32[]{:S(2)}, u32[]{:S(2)}) collective-permute-start(bf16[128,896]{1,0:T(8,128)(2,1)S(1)} %fusion.179), channel_id=1, source_target_pairs={{8,0},{10,2},{16,8},{18,10},{24,16},{26,18},{28,24},{30,26},{20,28... | collective-permute-start | bytes 688136 | tf_op jit(solution)/shard_map/ppermute | solution.py:94
  331.5 21.4 %collective-permute-start.46 = (bf16[128,896]{1,0:T(8,128)(2,1)S(1)}, bf16[128,896]{1,0:T(8,128)(2,1)S(1)}, u32[]{:S(2)}, u32[]{:S(2)}) collective-permute-start(bf16[128,896]{1,0:T(8,128)(2,1)S(1)} %fusion.184), channel_id=1, source_target_pairs={{8,0},{10,2},{16,8},{18,10},{24,16},{26,18},{28,24},{30,26},{20,28... | collective-permute-start | bytes 688136 | tf_op jit(solution)/shard_map/ppermute | solution.py:94
  434.4 23.4 %collective-permute-start.82 = (bf16[464,1024]{1,0:T(8,128)(2,1)}, bf16[464,1024]{1,0:T(8,128)(2,1)}, u32[]{:S(2)}, u32[]{:S(2)}) collective-permute-start(bf16[464,1024]{1,0:T(8,128)(2,1)} %copy.187), channel_id=1, source_target_pairs={{0,1},{1,0},{2,3},{3,2},{4,5},{5,4},{6,7},{7,6},{8,9},{9,8},{10,11... | collective-permute-start | bytes 2850824 | tf_op jit(solution)/shard_map/ppermute | solution.py:269
  473.1 11.4 %collective-permute-start.72 = (bf16[8,128,256]{2,1,0:T(8,128)(2,1)}, bf16[8,128,256]{2,1,0:T(8,128)(2,1)}, u32[]{:S(2)}, u32[]{:S(2)}) collective-permute-start(bf16[8,128,256]{2,1,0:T(8,128)(2,1)} %bitcast.71), channel_id=1, source_target_pairs={{0,2},{2,0},{4,6},{6,4},{8,10},{10,8},{12,14},{14,12},{16,18},{18,... | collective-permute-start | bytes 1572872 | tf_op jit(solution)/shard_map/ppermute | solution.py:97
  476.3 6.2 collective-permute-start.84
  478.0 7.6 %collective-permute-start.88 = (bf16[464,128]{0,1:T(8,128)(2,1)S(1)}, bf16[464,128]{0,1:T(8,128)(2,1)S(1)}, u32[]{:S(2)}, u32[]{:S(2)}) collective-permute-start(bf16[464,128]{0,1:T(8,128)(2,1)S(1)} %pad_maximum_fusion.19), channel_id=1, source_target_pairs={{8,0},{10,2},{16,8},{18,10},{24,16},{26,18},{28,24},{30,26},{20,28... | collective-permute-start | bytes 356360 | tf_op jit(solution)/shard_map/ppermute | solution.py:94
  499.7 6.6 %collective-permute-start.91 = (bf16[464,128]{0,1:T(8,128)(2,1)S(1)}, bf16[464,128]{0,1:T(8,128)(2,1)S(1)}, u32[]{:S(2)}, u32[]{:S(2)}) collective-permute-start(bf16[464,128]{0,1:T(8,128)(2,1)S(1)} %fusion.204), channel_id=1, source_target_pairs={{0,8},{2,10},{8,16},{10,18},{16,24},{18,26},{24,28},{26,30},{28,20... | collective-permute-start | bytes 356360 | tf_op jit(solution)/shard_map/ppermute | solution.py:91
  501.0 6.4 collective-permute-start.92
  502.3 6.3 collective-permute-start.74
  503.1 11.7 %collective-permute-start.78 = (bf16[128,256]{1,0:T(8,128)(2,1)S(1)}, bf16[128,256]{1,0:T(8,128)(2,1)S(1)}, u32[]{:S(2)}, u32[]{:S(2)}) collective-permute-start(bf16[128,256]{1,0:T(8,128)(2,1)S(1)} %pad_maximum_fusion.21), channel_id=1, source_target_pairs={{8,0},{10,2},{16,8},{18,10},{24,16},{26,18},{28,24},{30,26},{20,28... | collective-permute-start | bytes 196616 | tf_op jit(solution)/shard_map/ppermute | solution.py:94
  507.3 6.4 collective-permute-start.94
  512.3 24.4 %collective-permute-start.95 = (bf16[464,128]{0,1:T(8,128)(2,1)S(1)}, bf16[464,128]{0,1:T(8,128)(2,1)S(1)}, u32[]{:S(2)}, u32[]{:S(2)}) collective-permute-start(bf16[464,128]{0,1:T(8,128)(2,1)S(1)} %collective-permute-done.93), channel_id=1, source_target_pairs={{0,8},{2,10},{8,16},{10,18},{16,24},{18,26},{24,28},{26,30},{28,20... | collective-permute-start | bytes 356360 | tf_op jit(solution)/shard_map/ppermute | solution.py:91
  513.7 21.0 %collective-permute-start.96 = (bf16[464,128]{0,1:T(8,128)(2,1)S(1)}, bf16[464,128]{0,1:T(8,128)(2,1)S(1)}, u32[]{:S(2)}, u32[]{:S(2)}) collective-permute-start(bf16[464,128]{0,1:T(8,128)(2,1)S(1)} %collective-permute-done.94), channel_id=1, source_target_pairs={{8,0},{10,2},{16,8},{18,10},{24,16},{26,18},{28,24},{30,26},{20,28... | collective-permute-start | bytes 356360 | tf_op jit(solution)/shard_map/ppermute | solution.py:94
  515.4 21.5 %collective-permute-start.79 = (bf16[128,256]{1,0:T(8,128)(2,1)S(1)}, bf16[128,256]{1,0:T(8,128)(2,1)S(1)}, u32[]{:S(2)}, u32[]{:S(2)}) collective-permute-start(bf16[128,256]{1,0:T(8,128)(2,1)S(1)} %get-tuple-element.651), channel_id=1, source_target_pairs={{8,0},{10,2},{16,8},{18,10},{24,16},{26,18},{28,24},{30,26},{20,28... | collective-permute-start | bytes 196616 | tf_op jit(solution)/shard_map/ppermute | solution.py:94
  534.5 57.8 %collective-permute-start.76 = (bf16[128,256]{1,0:T(8,128)(2,1)}, bf16[128,256]{1,0:T(8,128)(2,1)S(1)}, u32[]{:S(2)}, u32[]{:S(2)}) collective-permute-start(bf16[128,256]{1,0:T(8,128)(2,1)} %get-tuple-element.650), channel_id=1, source_target_pairs={{0,8},{2,10},{8,16},{10,18},{16,24},{18,26},{24,28},{26,30},{28,20... | collective-permute-start | bytes 196616 | tf_op jit(solution)/shard_map/ppermute | solution.py:91
  534.8 50.7 %collective-permute-start.98 = (bf16[232,128]{0,1:T(8,128)(2,1)S(1)}, bf16[232,128]{0,1:T(8,128)(2,1)S(1)}, u32[]{:S(2)}, u32[]{:S(2)}) collective-permute-start(bf16[232,128]{0,1:T(8,128)(2,1)S(1)} %slice.852), channel_id=1, source_target_pairs={{8,0},{10,2},{16,8},{18,10},{24,16},{26,18},{28,24},{30,26},{20,28... | collective-permute-start | bytes 178184 | tf_op jit(solution)/shard_map/ppermute | solution.py:94
  536.7 48.8 %collective-permute-start.97 = (bf16[232,128]{0,1:T(8,128)(2,1)S(1)}, bf16[232,128]{0,1:T(8,128)(2,1)S(1)}, u32[]{:S(2)}, u32[]{:S(2)}) collective-permute-start(bf16[232,128]{0,1:T(8,128)(2,1)S(1)} %slice.851), channel_id=1, source_target_pairs={{0,8},{2,10},{8,16},{10,18},{16,24},{18,26},{24,28},{26,30},{28,20... | collective-permute-start | bytes 178184 | tf_op jit(solution)/shard_map/ppermute | solution.py:91
  537.8 54.5 %collective-permute-start.80 = (bf16[128,256]{1,0:T(8,128)(2,1)S(1)}, bf16[128,256]{1,0:T(8,128)(2,1)S(1)}, u32[]{:S(2)}, u32[]{:S(2)}) collective-permute-start(bf16[128,256]{1,0:T(8,128)(2,1)S(1)} %fusion.222), channel_id=1, source_target_pairs={{8,0},{10,2},{16,8},{18,10},{24,16},{26,18},{28,24},{30,26},{20,28... | collective-permute-start | bytes 196616 | tf_op jit(solution)/shard_map/ppermute | solution.py:94
  (123 other events, 1287.1 us)
Sparse Core Ops, SparseCore 0:
  265.8 130.5 all-gather.1
